TPU v7x, 1024 devices: a whole 8x8x8 slice. The times are simulated.
1024 devices in a mesh: seq: 64 (over z, y), head: 16 (over x, core).
Axes of the slice: x: 8, y: 8, z: 8, core: 2. Of those that a mesh axis runs over, the one named last changes fastest.
Arguments:
- queries: bfloat16 [32768, 6144], P('seq', 'head'), may hold values from -6 to 6
- keys: bfloat16 [32768, 6144], P('seq', 'head'), may hold values from -6 to 6
- values: bfloat16 [32768, 6144], P('seq', 'head'), may hold values from -6 to 6
- attn_out: bfloat16 [32768, 6144], P('seq', 'head'), may hold values from -120 to 120
- out_grad: bfloat16 [32768, 6144], P('seq', 'head'), may hold values from -6 to 6
- norm_gain: float32 [6144], P('head'), may hold values from 0.5 to 2
Outputs:
- query_grad: bfloat16 [32768, 6144], P('seq', 'head')
- key_grad: bfloat16 [32768, 6144], P('seq', 'head')
- value_grad: bfloat16 [32768, 6144], P('seq', 'head')
All inputs are finite; a program needn't handle non-finite values.
Results may differ from a plain program's by a relative error of at most 0.0057.
Values sent between devices are 32-bit elements; how exact they have to be, the bound alone decides.
No kernel may reach another device: no remote copies, remote signals or barrier semaphores. Data moves between devices by JAX's collectives and lax.ppermute only.
A program may use at most 64 MiB of HBM per device.

v0:
```python
import math

import jax
import jax.numpy as jnp
from jax import lax
from jax.sharding import PartitionSpec as P

DH = 128
GROUP = 256


EPS = 1e-06


def prefix(part, axis, combine, identity, reverse):
    count = lax.axis_size(axis)
    place = lax.axis_index(axis)
    ahead = count - 1 - place if reverse else place
    gathered = lax.all_gather(part, axis)
    state = jnp.zeros_like(part) + jnp.asarray(identity, part.dtype)

    def one(hop, state):
        source = count - 1 - hop if reverse else hop
        return combine(state, lax.dynamic_index_in_dim(gathered, source, 0, False))

    return lax.fori_loop(0, ahead, one, state)


def add_arrays(earlier, later):
    return earlier + later


def shards(queries, keys, values, attn_out, out_grad, norm_gain):
    tokens_here, width = queries.shape
    heads_here = width // DH
    full_width = width * lax.axis_size("head")
    tokens_all = tokens_here * lax.axis_size("seq")
    factor = 1.0 / math.sqrt(DH * tokens_all)
    outf = attn_out.astype(jnp.float32)
    scaled = norm_gain[None, :] * out_grad.astype(jnp.float32)
    square_part = jnp.sum(outf * outf, axis=-1)
    cross_part = jnp.sum(scaled * outf, axis=-1)
    square_sum, cross_sum = lax.psum((square_part, cross_part), "head")
    rms = jnp.sqrt(square_sum / full_width + EPS)
    grad_out = (
        scaled / rms[:, None] - outf * (cross_sum / (full_width * rms**3))[:, None]
    ).astype(jnp.bfloat16)
    blocks = tokens_here // GROUP
    shape = (blocks, GROUP, heads_here, DH)
    qb = queries.reshape(shape)
    kb = keys.reshape(shape)
    vb = values.reshape(shape)
    gb = grad_out.reshape(shape)
    f32 = jnp.float32
    kv_terms = jnp.einsum("ctni,ctnj->cnij", kb, vb, preferred_element_type=f32)
    qg_terms = jnp.einsum("ctni,ctnj->cnij", qb, gb, preferred_element_type=f32)
    kv_sum = jnp.sum(kv_terms, axis=0)
    qg_sum = jnp.sum(qg_terms, axis=0)
    zeros = jnp.zeros_like(kv_sum)
    before = prefix(kv_sum, "seq", add_arrays, zeros, False)
    after = prefix(qg_sum, "seq", add_arrays, zeros, True)
    fwd_state = (before[None] + jnp.cumsum(kv_terms, axis=0) - kv_terms).astype(jnp.bfloat16)
    bwd_state = (after[None] + qg_sum[None] - jnp.cumsum(qg_terms, axis=0)).astype(jnp.bfloat16)
    causal = (jnp.arange(GROUP)[:, None] >= jnp.arange(GROUP)[None, :])[None, None]
    scores = jnp.einsum("ctni,csni->cnts", qb, kb, preferred_element_type=f32)
    scores = jnp.where(causal, scores, 0.0).astype(jnp.bfloat16)
    prods = jnp.einsum("ctnj,csnj->cnts", gb, vb, preferred_element_type=f32)
    prods = jnp.where(causal, prods, 0.0).astype(jnp.bfloat16)
    qgrad = jnp.einsum("cnts,csni->ctni", prods, kb, preferred_element_type=f32)
    qgrad = qgrad + jnp.einsum("ctnj,cnij->ctni", gb, fwd_state, preferred_element_type=f32)
    kgrad = jnp.einsum("cnts,ctni->csni", prods, qb, preferred_element_type=f32)
    kgrad = kgrad + jnp.einsum("csnj,cnij->csni", vb, bwd_state, preferred_element_type=f32)
    vgrad = jnp.einsum("cnts,ctnj->csnj", scores, gb, preferred_element_type=f32)
    vgrad = vgrad + jnp.einsum("csni,cnij->csnj", kb, bwd_state, preferred_element_type=f32)
    query_grad = (qgrad * factor).astype(jnp.bfloat16).reshape(tokens_here, width)
    key_grad = (kgrad * factor).astype(jnp.bfloat16).reshape(tokens_here, width)
    value_grad = (vgrad * factor).astype(jnp.bfloat16).reshape(tokens_here, width)
    return (query_grad, key_grad, value_grad)


def solution(mesh):
    in_specs = (
        P("seq", "head"),
        P("seq", "head"),
        P("seq", "head"),
        P("seq", "head"),
        P("seq", "head"),
        P("head"),
    )
    out_specs = (P("seq", "head"), P("seq", "head"), P("seq", "head"))
    return jax.shard_map(shards, mesh=mesh, in_specs=in_specs, out_specs=out_specs, check_vma=False)
```

profile of v0, /device:TPU:1009, one launch (start us, length us, event | category | flops | bytes accessed | tf_op | source)
XLA Modules:
  0.0 361.4 jit_solution(16616403340725686418)
XLA Ops:
  7.2 1.4 fusion.14
  8.6 23.7 %all-reduce = (f32[512]{0:T(512)S(1)}, f32[512]{0:T(512)S(1)}) all-reduce(f32[512]{0:T(512)S(1)} %get-tuple-element.91, f32[512]{0:T(512)S(1)} %get-tuple-element.90), channel_id=1, replica_groups=mesh['seq'=64,'head'=16] {'head'}, use_global_device_ids=true, to_apply=%region_3.0 | all-reduce | flops 1024 | bytes 8192 | tf_op jit(solution)/shard_map/psum | solution.py:43
  32.4 1.4 fusion.17
  34.3 1.0 fusion.32
  38.1 121.1 %all-gather.7.cloned.1.call-done = f32[192,128,128]{2,1,0:T(8,128)} async-done(((f32[3,128,128]{2,1,0:T(8,128)}), f32[192,128,128]{2,1,0:T(8,128)}) %all-gather.7.cloned.1.call-update) | async-done | bytes 12582928 | tf_op jit(solution)/shard_map/all_gather | solution.py:19
  161.0 1.0 fusion.13
  163.1 1.2 fusion.33
  164.2 1.6 fusion.11
  165.9 1.1 copy.89
  167.0 121.5 %all-gather.5.cloned.1.call-done = f32[192,128,128]{2,1,0:T(8,128)} async-done(((f32[3,128,128]{2,1,0:T(8,128)}), f32[192,128,128]{2,1,0:T(8,128)}) %all-gather.5.cloned.1.call-update) | async-done | bytes 12582928 | tf_op jit(solution)/shard_map/all_gather | solution.py:19
  288.5 63.2 %while.22 = (s32[]{:T(128)}, f32[3,128,128]{2,1,0:T(8,128)S(1)}, s32[]{:T(128)}, f32[64,3,128,128]{3,2,1,0:T(8,128)}, s32[]{:T(128)}, /*index=5*/s32[]{:T(128)}, s32[]{:T(128)}) while((s32[]{:T(128)}, f32[3,128,128]{2,1,0:T(8,128)S(1)}, s32[]{:T(128)}, f32[64,3,128,128]{3,2,1,0:T(8,128)}, s32[]{:T(128)}, /*index=5*/s32[]{:T(128)}, ...), condition=%wide.region_6.7_spmd, body=%wide.region_5.0_spmd.sunk | while | flops 49157 | bytes 589939 | solution.py:26
  288.5 1.0 bitcast_add_fusion.4
  289.5 1.0 bitcast_add_fusion.4
  290.5 1.0 bitcast_add_fusion.4
  291.5 1.0 bitcast_add_fusion.4
  292.5 1.0 bitcast_add_fusion.4
  293.6 1.0 bitcast_add_fusion.4
  294.6 1.0 bitcast_add_fusion.4
  295.6 1.0 bitcast_add_fusion.4
  296.6 1.0 bitcast_add_fusion.4
  297.6 1.0 bitcast_add_fusion.4
  298.6 1.0 bitcast_add_fusion.4
  299.6 1.0 bitcast_add_fusion.4
  300.6 1.0 bitcast_add_fusion.4
  301.6 1.0 bitcast_add_fusion.4
  302.6 1.0 bitcast_add_fusion.4
  303.6 1.0 bitcast_add_fusion.4
  304.6 1.0 bitcast_add_fusion.4
  305.6 1.0 bitcast_add_fusion.4
  306.6 1.0 bitcast_add_fusion.4
  307.6 1.0 bitcast_add_fusion.4
  308.6 1.0 bitcast_add_fusion.4
  309.6 1.0 bitcast_add_fusion.4
  310.6 1.0 bitcast_add_fusion.4
  311.6 1.0 bitcast_add_fusion.4
  312.6 1.0 bitcast_add_fusion.4
  313.6 1.0 bitcast_add_fusion.4
  314.6 1.0 bitcast_add_fusion.4
  315.6 1.0 bitcast_add_fusion.4
  316.6 1.0 bitcast_add_fusion.4
  317.6 1.0 bitcast_add_fusion.4
  318.6 1.0 bitcast_add_fusion.4
  319.6 1.0 bitcast_add_fusion.4
  320.6 1.0 bitcast_add_fusion.4
  321.6 1.0 bitcast_add_fusion.4
  322.6 1.0 bitcast_add_fusion.4
  323.6 1.0 bitcast_add_fusion.4
  324.6 1.0 bitcast_add_fusion.4
  325.6 1.0 bitcast_add_fusion.4
  326.6 1.0 bitcast_add_fusion.4
  327.6 1.0 bitcast_add_fusion.4
  328.6 1.0 bitcast_add_fusion.4
  329.6 1.0 bitcast_add_fusion.4
  331.7 1.0 bitcast_add_fusion.4
  333.7 1.0 bitcast_add_fusion.4
  336.7 1.0 bitcast_add_fusion.4
  338.7 1.0 bitcast_add_fusion.4
  340.7 1.0 bitcast_add_fusion.4
  341.7 1.0 bitcast_add_fusion.4
  343.7 1.0 bitcast_add_fusion.4
  345.7 1.0 bitcast_add_fusion.4
  348.7 1.0 bitcast_add_fusion.4
  350.7 1.0 bitcast_add_fusion.4
  353.6 1.0 copy_bitcast_fusion
  (47 shorter events, 18.7 us)
Async XLA Ops:
  7.2 152.0 %all-gather.7.cloned.1.call-start = ((), (), s32[]{:S(2)}) async-start(), calls=%async_computation.1 | async-start | bytes 12779520 | tf_op jit(solution)/shard_map/all_gather | solution.py:19
  8.6 25.5 %copy-start.1 = (bf16[512,384]{1,0:T(8,128)(2,1)S(1)}, bf16[512,384]{1,0:T(8,128)(2,1)}, u32[]{:S(2)}) copy-start(bf16[512,384]{1,0:T(8,128)(2,1)} %param.10) | copy-start | bytes 1179652
  34.1 2.0 copy-start.2
  34.2 2.0 copy-start.3
  36.1 252.4 %all-gather.5.cloned.1.call-start = ((), (), s32[]{:S(2)}) async-start(), calls=%async_computation | async-start | bytes 12779520 | tf_op jit(solution)/shard_map/all_gather | solution.py:19
  352.1 1.5 copy-start
Sparse Core Ops, SparseCore 0:
  36.2 122.9 all-gather.6
  163.9 124.5 all-gather.4
where the time goes:
time: 363 us; the launch traced here: 361 us
  waiting for transfers between devices  243 us (67%)
  other arithmetic  66.3 us (18%)
  blocking collectives  23.7 us (7%)
  between operations  14.2 us (4%)
  matrix products  6.55 us (2%)
  local copies, waits for them, and re-layouts  6.15 us (2%)
    all_gather x2, waiting for transfers between devices, prefix(): gathered = lax.all_gather(part, axis)  243 us
    add x63, other arithmetic, add_arrays(): return earlier + later  61.5 us
    psum x1, blocking collectives, shards(): square_sum, cross_sum = lax.psum((square_part, cross_part), 'head')  23.7 us
  transfers between devices with their start and end apart: 2, of which 2 were waited for; matrix products, arithmetic and copies ran while one was open for 3% of the time, Pallas kernels for 0%

commit v1 on v0

v1 whole, which is shorter than its diff:
```python
import functools
import math

import jax
import jax.numpy as jnp
from jax import lax
from jax.experimental import pallas as pl
from jax.experimental.pallas import tpu as pltpu
from jax.sharding import PartitionSpec as P

DH = 128
GROUP = 256
EPS = 1e-06
F32 = jnp.float32
BF16 = jnp.bfloat16
VMEM = pl.BlockSpec(memory_space=pltpu.VMEM)


def dot(a, b, contract):
    return lax.dot_general(a, b, (contract, ((), ())), preferred_element_type=F32)


NN = ((1,), (0,))
NT = ((1,), (1,))
TN = ((0,), (0,))


def stats_kernel(out_ref, grad_ref, gain_ref, send_ref):
    tokens, width = out_ref.shape
    rows = tokens // DH
    gain = gain_ref[...].reshape(1, width)
    squares, crosses = [], []
    for r in range(rows):
        o = out_ref[pl.ds(r * DH, DH), :].astype(F32)
        s = grad_ref[pl.ds(r * DH, DH), :].astype(F32) * gain
        oo, so = o * o, s * o
        sq, cr = oo[:, :DH], so[:, :DH]
        for h in range(1, width // DH):
            sq = sq + oo[:, h * DH : (h + 1) * DH]
            cr = cr + so[:, h * DH : (h + 1) * DH]
        squares.append(jnp.sum(sq.T, axis=0, keepdims=True))
        crosses.append(jnp.sum(cr.T, axis=0, keepdims=True))
    block = jnp.concatenate(squares + crosses, axis=0)
    for copy in range(send_ref.shape[0]):
        send_ref[copy] = block


def grad_out_kernel(full_width, parts_ref, out_ref, grad_ref, gain_ref, q_ref, k_ref, v_ref,
                    g_ref, state_ref, kv0_ref, qg1_ref):
    tokens, width = out_ref.shape
    heads = width // DH
    rows = tokens // DH
    total = parts_ref[0]
    for d in range(1, parts_ref.shape[0]):
        total = total + parts_ref[d]
    inv = lax.rsqrt(total[:rows] / full_width + EPS)
    coef = total[rows:] * (inv * inv * inv) / full_width
    columns = jnp.concatenate([inv, coef], axis=0).T
    gain = gain_ref[...].reshape(1, width)
    for r in range(rows):
        here = pl.ds(r * DH, DH)
        s = grad_ref[here, :].astype(F32) * gain
        o = out_ref[here, :].astype(F32)
        g = s * columns[:, r : r + 1] - o * columns[:, rows + r : rows + r + 1]
        g_ref[here, :] = g.astype(BF16)
    half = heads * DH
    for h in range(heads):
        cols = pl.ds(h * DH, DH)
        kv, qg = [], []
        for b in range(2):
            here = pl.ds(b * GROUP, GROUP)
            kv.append(dot(k_ref[here, cols], v_ref[here, cols], TN))
            qg.append(dot(q_ref[here, cols], g_ref[here, cols], TN))
        kv0_ref[pl.ds(h * DH, DH), :] = kv[0]
        qg1_ref[pl.ds(h * DH, DH), :] = qg[1]
        state_ref[pl.ds(h * DH, DH), :] = kv[0] + kv[1]
        state_ref[pl.ds(half + h * DH, DH), :] = qg[0] + qg[1]


def scan_kernel(count, x_ref, y_ref):
    step = x_ref.shape[0] // count
    forward = lax.axis_index("seq") < count // 2

    def scan(order):
        total = jnp.zeros((step, x_ref.shape[1]), F32)
        for p in order:
            y_ref[p * step : (p + 1) * step, :] = total
            total = total + x_ref[p * step : (p + 1) * step, :]

    @pl.when(forward)
    def _():
        scan(range(count))

    @pl.when(jnp.logical_not(forward))
    def _():
        scan(range(count - 1, -1, -1))


def output_kernel(factor, carry_ref, kv0_ref, qg1_ref, q_ref, k_ref, v_ref, g_ref,
                  qgrad_ref, kgrad_ref, vgrad_ref):
    width = q_ref.shape[1]
    heads = width // DH
    half = heads * DH
    row = lax.broadcasted_iota(jnp.int32, (GROUP, GROUP), 0)
    col = lax.broadcasted_iota(jnp.int32, (GROUP, GROUP), 1)
    lower = row >= col
    upper = row <= col
    for h in range(heads):
        cols = pl.ds(h * DH, DH)
        before = carry_ref[pl.ds(h * DH, DH), :]
        after = carry_ref[pl.ds(half + h * DH, DH), :]
        for b in range(2):
            here = pl.ds(b * GROUP, GROUP)
            q, k, v, g = q_ref[here, cols], k_ref[here, cols], v_ref[here, cols], g_ref[here, cols]
            if b == 0:
                fwd = before
                bwd = after + qg1_ref[pl.ds(h * DH, DH), :]
            else:
                fwd = before + kv0_ref[pl.ds(h * DH, DH), :]
                bwd = after
            fwd, bwd = fwd.astype(BF16), bwd.astype(BF16)
            prods = jnp.where(lower, dot(g, v, NT), 0.0).astype(BF16)
            prods_t = jnp.where(upper, dot(v, g, NT), 0.0).astype(BF16)
            scores_t = jnp.where(upper, dot(k, q, NT), 0.0).astype(BF16)
            qgrad = dot(prods, k, NN) + dot(g, fwd, NT)
            kgrad = dot(prods_t, q, NN) + dot(v, bwd, NT)
            vgrad = dot(scores_t, g, NN) + dot(k, bwd, NN)
            qgrad_ref[here, cols] = (qgrad * factor).astype(BF16)
            kgrad_ref[here, cols] = (kgrad * factor).astype(BF16)
            vgrad_ref[here, cols] = (vgrad * factor).astype(BF16)


def shards(queries, keys, values, attn_out, out_grad, norm_gain):
    tokens, width = queries.shape
    n_head, n_seq = lax.axis_size("head"), lax.axis_size("seq")
    full_width = width * n_head
    factor = 1.0 / math.sqrt(DH * tokens * n_seq)
    shape = jax.ShapeDtypeStruct
    params = pltpu.CompilerParams(vmem_limit_bytes=16 << 20)
    call = functools.partial(pl.pallas_call, compiler_params=params)
    send = call(
        stats_kernel,
        in_specs=[VMEM] * 3,
        out_specs=VMEM,
        out_shape=shape((n_head, 2 * tokens // DH, DH), F32),
        name="stats",
    )(attn_out, out_grad, norm_gain)
    parts = lax.all_to_all(send, "head", 0, 0)
    g, state, kv0, qg1 = call(
        functools.partial(grad_out_kernel, full_width),
        in_specs=[VMEM] * 7,
        out_specs=[VMEM] * 4,
        out_shape=[
            shape((tokens, width), BF16),
            shape((2 * width, DH), F32),
            shape((width, DH), F32),
            shape((width, DH), F32),
        ],
        name="grad_out",
    )(parts, attn_out, out_grad, norm_gain, queries, keys, values)
    piece = 2 * width * DH // n_seq
    gathered = lax.all_to_all(state.reshape(n_seq, 1, piece), "seq", 0, 0)
    scanned = call(
        functools.partial(scan_kernel, n_seq),
        in_specs=[VMEM],
        out_specs=VMEM,
        out_shape=shape((2 * width, DH), F32),
        name="scan",
    )(gathered.reshape(2 * width, DH))
    carry = lax.all_to_all(scanned.reshape(n_seq, 1, piece), "seq", 0, 0)
    return call(
        functools.partial(output_kernel, factor),
        in_specs=[VMEM] * 7,
        out_specs=[VMEM] * 3,
        out_shape=[shape((tokens, width), BF16)] * 3,
        name="outputs",
    )(carry.reshape(2 * width, DH), kv0, qg1, queries, keys, values, g)


def solution(mesh):
    spec = P("seq", "head")
    return jax.shard_map(
        shards,
        mesh=mesh,
        in_specs=(spec,) * 5 + (P("head"),),
        out_specs=(spec,) * 3,
        check_vma=False,
    )
```

time: 363 us -> 84.7 us (0.23)
  the two profiles are of different devices: /device:TPU:1009 before, /device:TPU:16 now
where the time goes in v1:
time: 84.7 us; the launch traced here: 84.4 us
  blocking collectives  76.3 us (90%)
  local copies, waits for them, and re-layouts  3.73 us (4%)
  Pallas kernels  3.71 us (4%)
    all_to_all x1, blocking collectives, shards(): gathered = lax.all_to_all(state.reshape(n_seq, 1, piece), 'seq', 0, 0)  40.3 us
    all_to_all x1, blocking collectives, shards(): carry = lax.all_to_all(scanned.reshape(n_seq, 1, piece), 'seq', 0, 0)  21.5 us
    all_to_all x1, blocking collectives, shards(): parts = lax.all_to_all(send, 'head', 0, 0)  14.5 us
    unnamed x14, local copies, waits for them, and re-layouts  3.73 us
    pallas_call x1, Pallas kernels, shards(): call(functools.partial(output_kernel, factor), in_specs=[VMEM] * 7, out_s...  2.64 us

profile of v1, /device:TPU:16, one launch (start us, length us, event | category | flops | bytes accessed | tf_op | source)
XLA Modules:
  0.0 84.4 jit_solution(1831001235349661131)
XLA Ops:
  0.6 0.0 copy-start.1
  0.6 0.0 copy-start.4
  0.7 1.0 %copy-done.4 = bf16[512,384]{1,0:T(8,128)(2,1)S(1)} copy-done((bf16[512,384]{1,0:T(8,128)(2,1)S(1)}, bf16[512,384]{1,0:T(8,128)(2,1)}, u32[]{:S(2)}) %copy-start.4) | copy-done | bytes 393240
  1.7 0.0 copy-start.5
  1.7 1.0 %copy-done.5 = bf16[512,384]{1,0:T(8,128)(2,1)S(1)} copy-done((bf16[512,384]{1,0:T(8,128)(2,1)S(1)}, bf16[512,384]{1,0:T(8,128)(2,1)}, u32[]{:S(2)}) %copy-start.5) | copy-done | bytes 393240
  2.7 0.0 copy-start.6
  2.7 0.7 copy-done.6
  3.4 0.0 copy-start
  3.4 0.3 stats.1
  3.6 14.5 %all_to_all.15.parts_ref = f32[16,8,128]{2,1,0:T(8,128)S(1)} all-to-all(f32[16,8,128]{2,1,0:T(8,128)S(1)} %stats.1), channel_id=1, replica_groups=mesh['seq'=64,'head'=16] {'head'}, dimensions={0} | all-to-all | bytes 131072 | tf_op jit(solution)/shard_map/all_to_all | solution.py:148
  18.2 0.0 copy-done.1
  18.2 0.0 copy-done
  18.2 0.0 copy-start.2
  18.2 1.0 %copy-done.2 = bf16[512,384]{1,0:T(8,128)(2,1)S(1)} copy-done((bf16[512,384]{1,0:T(8,128)(2,1)S(1)}, bf16[512,384]{1,0:T(8,128)(2,1)}, u32[]{:S(2)}) %copy-start.2) | copy-done | bytes 393240
  19.2 0.8 grad_out.1
  19.9 40.3 %all_to_all.16 = f32[64,1,1536]{2,1,0:T(1,128)S(1)} all-to-all(f32[64,1,1536]{2,1,0:T(1,128)S(1)} %bitcast.7), channel_id=1, replica_groups=mesh['seq'=64,'head'=16] {'seq'}, dimensions={0} | all-to-all | bytes 786432 | tf_op jit(solution)/shard_map/all_to_all | solution.py:162
  60.2 0.1 scan.1
  60.3 0.0 copy-start.3
  60.3 21.5 %all_to_all.17 = f32[64,1,1536]{2,1,0:T(1,128)S(1)} all-to-all(f32[64,1,1536]{2,1,0:T(1,128)S(1)} %bitcast.6), channel_id=1, replica_groups=mesh['seq'=64,'head'=16] {'seq'}, dimensions={0} | all-to-all | bytes 786432 | tf_op jit(solution)/shard_map/all_to_all | solution.py:170
  81.8 0.0 copy-done.3
  81.8 2.6 %outputs.1 = (bf16[512,384]{1,0:T(8,128)(2,1)}, bf16[512,384]{1,0:T(8,128)(2,1)}, bf16[512,384]{1,0:T(8,128)(2,1)}) custom-call(f32[768,128]{1,0:T(8,128)S(1)} %bitcast.4, f32[384,128]{1,0:T(8,128)S(1)} %get-tuple-element.8.kv0_ref, f32[384,128]{1,0:T(8,128)S(1)} %get-tuple-element.9.qg1_ref, bf16[512,384]{1,0:T(8,128)(2,1)S(1)} %copy-done, ...), custom_call_target="tpu_custom_call" | custom-call | tf_op jit(solution)/shard_map/outputs/pallas_call | solution.py:171
Async XLA Ops:
  0.6 17.5 %copy-start.1 = (bf16[512,384]{1,0:T(8,128)(2,1)S(1)}, bf16[512,384]{1,0:T(8,128)(2,1)}, u32[]{:S(2)}) copy-start(bf16[512,384]{1,0:T(8,128)(2,1)} %k_ref.3) | copy-start | bytes 1179652
  0.6 1.0 %copy-start.4 = (bf16[512,384]{1,0:T(8,128)(2,1)S(1)}, bf16[512,384]{1,0:T(8,128)(2,1)}, u32[]{:S(2)}) copy-start(bf16[512,384]{1,0:T(8,128)(2,1)} %out_ref.3) | copy-start | bytes 1179652
  1.7 1.0 %copy-start.5 = (bf16[512,384]{1,0:T(8,128)(2,1)S(1)}, bf16[512,384]{1,0:T(8,128)(2,1)}, u32[]{:S(2)}) copy-start(bf16[512,384]{1,0:T(8,128)(2,1)} %grad_ref.3) | copy-start | bytes 1179652
  2.7 0.7 copy-start.6
  3.4 14.8 %copy-start = (bf16[512,384]{1,0:T(8,128)(2,1)S(1)}, bf16[512,384]{1,0:T(8,128)(2,1)}, u32[]{:S(2)}) copy-start(bf16[512,384]{1,0:T(8,128)(2,1)} %q_ref.3) | copy-start | bytes 1179652
  18.2 1.0 %copy-start.2 = (bf16[512,384]{1,0:T(8,128)(2,1)S(1)}, bf16[512,384]{1,0:T(8,128)(2,1)}, u32[]{:S(2)}) copy-start(bf16[512,384]{1,0:T(8,128)(2,1)} %v_ref.3) | copy-start | bytes 1179652
  60.3 21.5 %copy-start.3 = (bf16[512,384]{1,0:T(8,128)(2,1)S(1)}, bf16[512,384]{1,0:T(8,128)(2,1)}, u32[]{:S(2)}) copy-start(bf16[512,384]{1,0:T(8,128)(2,1)} %v_ref.3) | copy-start | bytes 1179652

commit v2 on v1

--- a/solution.py
+++ b/solution.py
@@ -14,6 +14,7 @@
 F32 = jnp.float32
 BF16 = jnp.bfloat16
 VMEM = pl.BlockSpec(memory_space=pltpu.VMEM)
+HBM = pl.BlockSpec(memory_space=pltpu.HBM)
 
 
 def dot(a, b, contract):
@@ -25,12 +26,30 @@
 TN = ((0,), (0,))
 
 
-def stats_kernel(out_ref, grad_ref, gain_ref, send_ref):
+def stats_kernel(out_hbm, grad_hbm, gain_hbm, v_hbm, send_ref, out_ref, grad_ref, gain_ref, v_ref, sems, gain_sem, v_sem):
     tokens, width = out_ref.shape
     rows = tokens // DH
+    copies = []
+    for r in range(rows):
+        here = pl.ds(r * DH, DH)
+        copies.append(
+            (
+                pltpu.make_async_copy(out_hbm.at[here], out_ref.at[here], sems.at[0, r]),
+                pltpu.make_async_copy(grad_hbm.at[here], grad_ref.at[here], sems.at[1, r]),
+            )
+        )
+    gain_copy = pltpu.make_async_copy(gain_hbm, gain_ref, gain_sem)
+    v_copy = pltpu.make_async_copy(v_hbm, v_ref, v_sem)
+    gain_copy.start()
+    for pair in copies:
+        pair[0].start()
+        pair[1].start()
+    v_copy.start()
+    gain_copy.wait()
     gain = gain_ref[...].reshape(1, width)
-    squares, crosses = [], []
     for r in range(rows):
+        copies[r][0].wait()
+        copies[r][1].wait()
         o = out_ref[pl.ds(r * DH, DH), :].astype(F32)
         s = grad_ref[pl.ds(r * DH, DH), :].astype(F32) * gain
         oo, so = o * o, s * o
@@ -38,11 +57,12 @@
         for h in range(1, width // DH):
             sq = sq + oo[:, h * DH : (h + 1) * DH]
             cr = cr + so[:, h * DH : (h + 1) * DH]
-        squares.append(jnp.sum(sq.T, axis=0, keepdims=True))
-        crosses.append(jnp.sum(cr.T, axis=0, keepdims=True))
-    block = jnp.concatenate(squares + crosses, axis=0)
-    for copy in range(send_ref.shape[0]):
-        send_ref[copy] = block
+        square = jnp.sum(sq.T, axis=0, keepdims=True)
+        cross = jnp.sum(cr.T, axis=0, keepdims=True)
+        for copy in range(send_ref.shape[0]):
+            send_ref[copy, r : r + 1, :] = square
+            send_ref[copy, rows + r : rows + r + 1, :] = cross
+    v_copy.wait()
 
 
 def grad_out_kernel(full_width, parts_ref, out_ref, grad_ref, gain_ref, q_ref, k_ref, v_ref,
@@ -64,17 +84,19 @@
         g = s * columns[:, r : r + 1] - o * columns[:, rows + r : rows + r + 1]
         g_ref[here, :] = g.astype(BF16)
     half = heads * DH
+
+    def terms(a_ref, b_ref, h):
+        cols = pl.ds(h * DH, DH)
+        return [dot(a_ref[pl.ds(b * GROUP, GROUP), cols], b_ref[pl.ds(b * GROUP, GROUP), cols], TN) for b in range(2)]
+
     for h in range(heads):
-        cols = pl.ds(h * DH, DH)
-        kv, qg = [], []
-        for b in range(2):
-            here = pl.ds(b * GROUP, GROUP)
-            kv.append(dot(k_ref[here, cols], v_ref[here, cols], TN))
-            qg.append(dot(q_ref[here, cols], g_ref[here, cols], TN))
+        qg = terms(q_ref, g_ref, h)
+        qg1_ref[pl.ds(h * DH, DH), :] = qg[1]
+        state_ref[pl.ds(half + h * DH, DH), :] = qg[0] + qg[1]
+    for h in range(heads):
+        kv = terms(k_ref, v_ref, h)
         kv0_ref[pl.ds(h * DH, DH), :] = kv[0]
-        qg1_ref[pl.ds(h * DH, DH), :] = qg[1]
         state_ref[pl.ds(h * DH, DH), :] = kv[0] + kv[1]
-        state_ref[pl.ds(half + h * DH, DH), :] = qg[0] + qg[1]
 
 
 def scan_kernel(count, x_ref, y_ref):
@@ -97,7 +119,8 @@
 
 
 def output_kernel(factor, carry_ref, kv0_ref, qg1_ref, q_ref, k_ref, v_ref, g_ref,
-                  qgrad_ref, kgrad_ref, vgrad_ref):
+                  qgrad_hbm, kgrad_hbm, vgrad_hbm, qgrad_ref, kgrad_ref, vgrad_ref, sems):
+    copies = []
     width = q_ref.shape[1]
     heads = width // DH
     half = heads * DH
@@ -125,9 +148,18 @@
             qgrad = dot(prods, k, NN) + dot(g, fwd, NT)
             kgrad = dot(prods_t, q, NN) + dot(v, bwd, NT)
             vgrad = dot(scores_t, g, NN) + dot(k, bwd, NN)
-            qgrad_ref[here, cols] = (qgrad * factor).astype(BF16)
-            kgrad_ref[here, cols] = (kgrad * factor).astype(BF16)
-            vgrad_ref[here, cols] = (vgrad * factor).astype(BF16)
+            results = (
+                (qgrad, qgrad_ref, qgrad_hbm),
+                (kgrad, kgrad_ref, kgrad_hbm),
+                (vgrad, vgrad_ref, vgrad_hbm),
+            )
+            for i, (value, ref, hbm) in enumerate(results):
+                ref[here, cols] = (value * factor).astype(BF16)
+                copy = pltpu.make_async_copy(ref.at[here, cols], hbm.at[here, cols], sems.at[i, b, h])
+                copy.start()
+                copies.append(copy)
+    for copy in copies:
+        copy.wait()
 
 
 def shards(queries, keys, values, attn_out, out_grad, norm_gain):
@@ -136,15 +168,27 @@
     full_width = width * n_head
     factor = 1.0 / math.sqrt(DH * tokens * n_seq)
     shape = jax.ShapeDtypeStruct
+    far = functools.partial(pltpu.with_memory_space_constraint, memory_space=pltpu.HBM)
     params = pltpu.CompilerParams(vmem_limit_bytes=16 << 20)
     call = functools.partial(pl.pallas_call, compiler_params=params)
-    send = call(
+    send, out_near, grad_near, gain_near, v_near = call(
         stats_kernel,
-        in_specs=[VMEM] * 3,
-        out_specs=VMEM,
-        out_shape=shape((n_head, 2 * tokens // DH, DH), F32),
+        in_specs=[HBM] * 4,
+        out_specs=[VMEM] * 5,
+        out_shape=[
+            shape((n_head, 2 * tokens // DH, DH), F32),
+            shape((tokens, width), BF16),
+            shape((tokens, width), BF16),
+            shape((width,), F32),
+            shape((tokens, width), BF16),
+        ],
+        scratch_shapes=[
+            pltpu.SemaphoreType.DMA((2, tokens // DH)),
+            pltpu.SemaphoreType.DMA,
+            pltpu.SemaphoreType.DMA,
+        ],
         name="stats",
-    )(attn_out, out_grad, norm_gain)
+    )(far(attn_out), far(out_grad), far(norm_gain), far(values))
     parts = lax.all_to_all(send, "head", 0, 0)
     g, state, kv0, qg1 = call(
         functools.partial(grad_out_kernel, full_width),
@@ -157,7 +201,7 @@
             shape((width, DH), F32),
         ],
         name="grad_out",
-    )(parts, attn_out, out_grad, norm_gain, queries, keys, values)
+    )(parts, out_near, grad_near, gain_near, queries, keys, v_near)
     piece = 2 * width * DH // n_seq
     gathered = lax.all_to_all(state.reshape(n_seq, 1, piece), "seq", 0, 0)
     scanned = call(
@@ -171,10 +215,12 @@
     return call(
         functools.partial(output_kernel, factor),
         in_specs=[VMEM] * 7,
-        out_specs=[VMEM] * 3,
+        out_specs=[HBM] * 3,
         out_shape=[shape((tokens, width), BF16)] * 3,
+        scratch_shapes=[pltpu.VMEM((tokens, width), BF16)] * 3
+        + [pltpu.SemaphoreType.DMA((3, tokens // GROUP, width // DH))],
         name="outputs",
-    )(carry.reshape(2 * width, DH), kv0, qg1, queries, keys, values, g)
+    )(carry.reshape(2 * width, DH), kv0, qg1, queries, keys, v_near, g)
 
 
 def solution(mesh):

time: 84.7 us -> 82.1 us (0.969)
  local copies, waits for them, and re-layouts: 3.73 us -> 0.01 us
  Pallas kernels: 3.71 us -> 5.05 us
    unnamed x14 -> x4, local copies, waits for them, and re-layouts: 3.73 us -> 0.01 us
    pallas_call x1, Pallas kernels: 0.25 us -> 1.66 us  [shards(): call(stats_kernel, in_specs=[HBM] * 4, out_specs=[VMEM] * 5, out_shape=[s...]
where the time goes in v2:
time: 82.1 us; the launch traced here: 81.9 us
  blocking collectives  76.2 us (93%)
  Pallas kernels  5.05 us (6%)
    all_to_all x1, blocking collectives, shards(): gathered = lax.all_to_all(state.reshape(n_seq, 1, piece), 'seq', 0, 0)  40.3 us
    all_to_all x1, blocking collectives, shards(): carry = lax.all_to_all(scanned.reshape(n_seq, 1, piece), 'seq', 0, 0)  21.4 us
    all_to_all x1, blocking collectives, shards(): parts = lax.all_to_all(send, 'head', 0, 0)  14.5 us
    pallas_call x1, Pallas kernels, shards(): call(functools.partial(output_kernel, factor), in_specs=[VMEM] * 7, out_s...  2.53 us
    pallas_call x1, Pallas kernels, shards(): call(stats_kernel, in_specs=[HBM] * 4, out_specs=[VMEM] * 5, out_shape=[s...  1.66 us

profile of v2, /device:TPU:16, one launch (start us, length us, event | category | flops | bytes accessed | tf_op | source)
XLA Modules:
  0.0 81.9 jit_solution(12756398605391886949)
XLA Ops:
  0.6 0.0 copy-start.1
  0.6 0.0 copy-start
  0.7 1.7 %stats.1 = (f32[16,8,128]{2,1,0:T(8,128)S(1)}, bf16[512,384]{1,0:T(8,128)(2,1)S(1)}, bf16[512,384]{1,0:T(8,128)(2,1)S(1)}, f32[384]{0:T(512)S(1)}, bf16[512,384]{1,0:T(8,128)(2,1)S(1)}) custom-call(bf16[512,384]{1,0:T(8,128)(2,1)} %out_hbm.1, bf16[512,384]{1,0:T(8,128)(2,1)} %grad_hbm.1, f32[384]{0:T(512)} %gain_hbm.1, bf16[512,384]{1,0:T(8,128)(2,1)} %v_hbm.1), custom_call_target="tpu_custom_call" | custom-call | tf_op jit(solution)/shard_map/stats/pallas_call | solution.py:174
  2.3 14.5 %all_to_all.15.parts_ref = f32[16,8,128]{2,1,0:T(8,128)S(1)} all-to-all(f32[16,8,128]{2,1,0:T(8,128)S(1)} %get-tuple-element.12), channel_id=1, replica_groups=mesh['seq'=64,'head'=16] {'head'}, dimensions={0} | all-to-all | bytes 131072 | tf_op jit(solution)/shard_map/all_to_all | solution.py:192
  16.9 0.0 copy-done.1
  16.9 0.0 copy-done
  16.9 0.8 grad_out.1
  17.7 40.3 %all_to_all.16 = f32[64,1,1536]{2,1,0:T(1,128)S(1)} all-to-all(f32[64,1,1536]{2,1,0:T(1,128)S(1)} %bitcast.7), channel_id=1, replica_groups=mesh['seq'=64,'head'=16] {'seq'}, dimensions={0} | all-to-all | bytes 786432 | tf_op jit(solution)/shard_map/all_to_all | solution.py:206
  57.9 0.1 scan.1
  58.0 21.4 %all_to_all.17 = f32[64,1,1536]{2,1,0:T(1,128)S(1)} all-to-all(f32[64,1,1536]{2,1,0:T(1,128)S(1)} %bitcast.6), channel_id=1, replica_groups=mesh['seq'=64,'head'=16] {'seq'}, dimensions={0} | all-to-all | bytes 786432 | tf_op jit(solution)/shard_map/all_to_all | solution.py:214
  79.4 2.5 %outputs.1 = (bf16[512,384]{1,0:T(8,128)(2,1)}, bf16[512,384]{1,0:T(8,128)(2,1)}, bf16[512,384]{1,0:T(8,128)(2,1)}) custom-call(f32[768,128]{1,0:T(8,128)S(1)} %bitcast.4, f32[384,128]{1,0:T(8,128)S(1)} %get-tuple-element.18.kv0_ref, f32[384,128]{1,0:T(8,128)S(1)} %get-tuple-element.19.qg1_ref, bf16[512,384]{1,0:T(8,128)(2,1)S(1)} %copy-done, ...), custom_call_target="tpu_custom_call" | custom-call | tf_op jit(solution)/shard_map/outputs/pallas_call | solution.py:215
Async XLA Ops:
  0.6 16.2 %copy-start.1 = (bf16[512,384]{1,0:T(8,128)(2,1)S(1)}, bf16[512,384]{1,0:T(8,128)(2,1)}, u32[]{:S(2)}) copy-start(bf16[512,384]{1,0:T(8,128)(2,1)} %k_ref.3) | copy-start | bytes 1179652
  0.6 16.2 %copy-start = (bf16[512,384]{1,0:T(8,128)(2,1)S(1)}, bf16[512,384]{1,0:T(8,128)(2,1)}, u32[]{:S(2)}) copy-start(bf16[512,384]{1,0:T(8,128)(2,1)} %q_ref.3) | copy-start | bytes 1179652

commit v3 on v2

--- a/solution.py
+++ b/solution.py
@@ -26,7 +26,21 @@
 TN = ((0,), (0,))
 
 
-def stats_kernel(out_hbm, grad_hbm, gain_hbm, v_hbm, send_ref, out_ref, grad_ref, gain_ref, v_ref, sems, gain_sem, v_sem):
+def early():
+    return lax.axis_index("seq") * 8 < lax.axis_size("seq") * 5
+
+
+def within_block(q, k, v, g):
+    row = lax.broadcasted_iota(jnp.int32, (GROUP, GROUP), 0)
+    col = lax.broadcasted_iota(jnp.int32, (GROUP, GROUP), 1)
+    prods = jnp.where(row >= col, dot(g, v, NT), 0.0).astype(BF16)
+    prods_t = jnp.where(row <= col, dot(v, g, NT), 0.0).astype(BF16)
+    scores_t = jnp.where(row <= col, dot(k, q, NT), 0.0).astype(BF16)
+    return dot(prods, k, NN), dot(prods_t, q, NN), dot(scores_t, g, NN)
+
+
+def stats_kernel(out_hbm, grad_hbm, gain_hbm, q_hbm, k_hbm, v_hbm,
+                 send_ref, out_ref, grad_ref, gain_ref, q_ref, k_ref, v_ref, sems, gain_sem, later_sems):
     tokens, width = out_ref.shape
     rows = tokens // DH
     copies = []
@@ -39,12 +53,16 @@
             )
         )
     gain_copy = pltpu.make_async_copy(gain_hbm, gain_ref, gain_sem)
-    v_copy = pltpu.make_async_copy(v_hbm, v_ref, v_sem)
+    later = [
+        pltpu.make_async_copy(hbm, ref, later_sems.at[i])
+        for i, (hbm, ref) in enumerate(((q_hbm, q_ref), (k_hbm, k_ref), (v_hbm, v_ref)))
+    ]
     gain_copy.start()
     for pair in copies:
         pair[0].start()
         pair[1].start()
-    v_copy.start()
+    for copy in later:
+        copy.start()
     gain_copy.wait()
     gain = gain_ref[...].reshape(1, width)
     for r in range(rows):
@@ -62,11 +80,12 @@
         for copy in range(send_ref.shape[0]):
             send_ref[copy, r : r + 1, :] = square
             send_ref[copy, rows + r : rows + r + 1, :] = cross
-    v_copy.wait()
+    for copy in later:
+        copy.wait()
 
 
 def grad_out_kernel(full_width, parts_ref, out_ref, grad_ref, gain_ref, q_ref, k_ref, v_ref,
-                    g_ref, state_ref, kv0_ref, qg1_ref):
+                    g_ref, state_ref, kv0_ref, qg1_ref, inner_ref):
     tokens, width = out_ref.shape
     heads = width // DH
     rows = tokens // DH
@@ -99,6 +118,16 @@
         state_ref[pl.ds(h * DH, DH), :] = kv[0] + kv[1]
 
 
+    @pl.when(early())
+    def _():
+        for h in range(heads):
+            for b in range(2):
+                here, cols = pl.ds(b * GROUP, GROUP), pl.ds(h * DH, DH)
+                tile = [ref[here, cols] for ref in (q_ref, k_ref, v_ref, g_ref)]
+                for i, value in enumerate(within_block(*tile)):
+                    inner_ref[i, here, cols] = value
+
+
 def scan_kernel(count, x_ref, y_ref):
     step = x_ref.shape[0] // count
     forward = lax.axis_index("seq") < count // 2
@@ -118,48 +147,51 @@
         scan(range(count - 1, -1, -1))
 
 
-def output_kernel(factor, carry_ref, kv0_ref, qg1_ref, q_ref, k_ref, v_ref, g_ref,
+def output_kernel(factor, carry_ref, kv0_ref, qg1_ref, q_ref, k_ref, v_ref, g_ref, inner_ref,
                   qgrad_hbm, kgrad_hbm, vgrad_hbm, qgrad_ref, kgrad_ref, vgrad_ref, sems):
-    copies = []
     width = q_ref.shape[1]
     heads = width // DH
     half = heads * DH
-    row = lax.broadcasted_iota(jnp.int32, (GROUP, GROUP), 0)
-    col = lax.broadcasted_iota(jnp.int32, (GROUP, GROUP), 1)
-    lower = row >= col
-    upper = row <= col
-    for h in range(heads):
-        cols = pl.ds(h * DH, DH)
-        before = carry_ref[pl.ds(h * DH, DH), :]
-        after = carry_ref[pl.ds(half + h * DH, DH), :]
+    results = ((qgrad_ref, qgrad_hbm), (kgrad_ref, kgrad_hbm), (vgrad_ref, vgrad_hbm))
+
+    def copy_of(i, b, h):
+        here, cols = pl.ds(b * GROUP, GROUP), pl.ds(h * DH, DH)
+        ref, hbm = results[i]
+        return pltpu.make_async_copy(ref.at[here, cols], hbm.at[here, cols], sems.at[i, b, h])
+
+    def finish(inner):
+        for h in range(heads):
+            cols = pl.ds(h * DH, DH)
+            before = carry_ref[pl.ds(h * DH, DH), :]
+            after = carry_ref[pl.ds(half + h * DH, DH), :]
+            for b in range(2):
+                here = pl.ds(b * GROUP, GROUP)
+                q, k, v, g = q_ref[here, cols], k_ref[here, cols], v_ref[here, cols], g_ref[here, cols]
+                if b == 0:
+                    fwd = before
+                    bwd = after + qg1_ref[pl.ds(h * DH, DH), :]
+                else:
+                    fwd = before + kv0_ref[pl.ds(h * DH, DH), :]
+                    bwd = after
+                fwd, bwd = fwd.astype(BF16), bwd.astype(BF16)
+                outer = dot(g, fwd, NT), dot(v, bwd, NT), dot(k, bwd, NN)
+                parts = inner(here, cols, (q, k, v, g))
+                for i in range(3):
+                    results[i][0][here, cols] = ((parts[i] + outer[i]) * factor).astype(BF16)
+                    copy_of(i, b, h).start()
+
+    @pl.when(early())
+    def _():
+        finish(lambda here, cols, tile: [inner_ref[i, here, cols] for i in range(3)])
+
+    @pl.when(jnp.logical_not(early()))
+    def _():
+        finish(lambda here, cols, tile: within_block(*tile))
+
+    for i in range(3):
         for b in range(2):
-            here = pl.ds(b * GROUP, GROUP)
-            q, k, v, g = q_ref[here, cols], k_ref[here, cols], v_ref[here, cols], g_ref[here, cols]
-            if b == 0:
-                fwd = before
-                bwd = after + qg1_ref[pl.ds(h * DH, DH), :]
-            else:
-                fwd = before + kv0_ref[pl.ds(h * DH, DH), :]
-                bwd = after
-            fwd, bwd = fwd.astype(BF16), bwd.astype(BF16)
-            prods = jnp.where(lower, dot(g, v, NT), 0.0).astype(BF16)
-            prods_t = jnp.where(upper, dot(v, g, NT), 0.0).astype(BF16)
-            scores_t = jnp.where(upper, dot(k, q, NT), 0.0).astype(BF16)
-            qgrad = dot(prods, k, NN) + dot(g, fwd, NT)
-            kgrad = dot(prods_t, q, NN) + dot(v, bwd, NT)
-            vgrad = dot(scores_t, g, NN) + dot(k, bwd, NN)
-            results = (
-                (qgrad, qgrad_ref, qgrad_hbm),
-                (kgrad, kgrad_ref, kgrad_hbm),
-                (vgrad, vgrad_ref, vgrad_hbm),
-            )
-            for i, (value, ref, hbm) in enumerate(results):
-                ref[here, cols] = (value * factor).astype(BF16)
-                copy = pltpu.make_async_copy(ref.at[here, cols], hbm.at[here, cols], sems.at[i, b, h])
-                copy.start()
-                copies.append(copy)
-    for copy in copies:
-        copy.wait()
+            for h in range(heads):
+                copy_of(i, b, h).wait()
 
 
 def shards(queries, keys, values, attn_out, out_grad, norm_gain):
@@ -171,37 +203,38 @@
     far = functools.partial(pltpu.with_memory_space_constraint, memory_space=pltpu.HBM)
     params = pltpu.CompilerParams(vmem_limit_bytes=16 << 20)
     call = functools.partial(pl.pallas_call, compiler_params=params)
-    send, out_near, grad_near, gain_near, v_near = call(
+    send, out_near, grad_near, gain_near, *near = call(
         stats_kernel,
-        in_specs=[HBM] * 4,
-        out_specs=[VMEM] * 5,
+        in_specs=[HBM] * 6,
+        out_specs=[VMEM] * 7,
         out_shape=[
             shape((n_head, 2 * tokens // DH, DH), F32),
             shape((tokens, width), BF16),
             shape((tokens, width), BF16),
             shape((width,), F32),
-            shape((tokens, width), BF16),
-        ],
+        ]
+        + [shape((tokens, width), BF16)] * 3,
         scratch_shapes=[
             pltpu.SemaphoreType.DMA((2, tokens // DH)),
             pltpu.SemaphoreType.DMA,
-            pltpu.SemaphoreType.DMA,
+            pltpu.SemaphoreType.DMA((3,)),
         ],
         name="stats",
-    )(far(attn_out), far(out_grad), far(norm_gain), far(values))
+    )(*map(far, (attn_out, out_grad, norm_gain, queries, keys, values)))
     parts = lax.all_to_all(send, "head", 0, 0)
-    g, state, kv0, qg1 = call(
+    g, state, kv0, qg1, inner = call(
         functools.partial(grad_out_kernel, full_width),
         in_specs=[VMEM] * 7,
-        out_specs=[VMEM] * 4,
+        out_specs=[VMEM] * 5,
         out_shape=[
             shape((tokens, width), BF16),
             shape((2 * width, DH), F32),
             shape((width, DH), F32),
             shape((width, DH), F32),
+            shape((3, tokens, width), F32),
         ],
         name="grad_out",
-    )(parts, out_near, grad_near, gain_near, queries, keys, v_near)
+    )(parts, out_near, grad_near, gain_near, *near)
     piece = 2 * width * DH // n_seq
     gathered = lax.all_to_all(state.reshape(n_seq, 1, piece), "seq", 0, 0)
     scanned = call(
@@ -214,13 +247,13 @@
     carry = lax.all_to_all(scanned.reshape(n_seq, 1, piece), "seq", 0, 0)
     return call(
         functools.partial(output_kernel, factor),
-        in_specs=[VMEM] * 7,
+        in_specs=[VMEM] * 8,
         out_specs=[HBM] * 3,
         out_shape=[shape((tokens, width), BF16)] * 3,
         scratch_shapes=[pltpu.VMEM((tokens, width), BF16)] * 3
         + [pltpu.SemaphoreType.DMA((3, tokens // GROUP, width // DH))],
         name="outputs",
-    )(carry.reshape(2 * width, DH), kv0, qg1, queries, keys, v_near, g)
+    )(carry.reshape(2 * width, DH), kv0, qg1, *near, g, inner)
 
 
 def solution(mesh):

time: 82.1 us -> 81.1 us (0.988)
  blocking collectives: 76.2 us -> 74.6 us
    pallas_call x1, Pallas kernels: 0.79 us -> 2.31 us  [shards(): call(functools.partial(grad_out_kernel, full_width), in_specs=[VMEM] * 7,...]
    all_to_all x1, blocking collectives: 40.3 us -> 38.7 us  [shards(): gathered = lax.all_to_all(state.reshape(n_seq, 1, piece), 'seq', 0, 0)]
    pallas_call x2, Pallas kernels: 4.2 us -> 3.22 us  [the longest x1 1.85 us: shards(): call(stats_kernel, in_specs=[HBM] * 6, out_specs=[VMEM] * 7, out_shape=[s...]
where the time goes in v3:
time: 81.1 us; the launch traced here: 80.9 us
  blocking collectives  74.6 us (92%)
  Pallas kernels  5.59 us (7%)
    all_to_all x1, blocking collectives, shards(): gathered = lax.all_to_all(state.reshape(n_seq, 1, piece), 'seq', 0, 0)  38.7 us
    all_to_all x1, blocking collectives, shards(): carry = lax.all_to_all(scanned.reshape(n_seq, 1, piece), 'seq', 0, 0)  21.4 us
    all_to_all x1, blocking collectives, shards(): parts = lax.all_to_all(send, 'head', 0, 0)  14.5 us
    pallas_call x1, Pallas kernels, shards(): call(functools.partial(grad_out_kernel, full_width), in_specs=[VMEM] * 7,...  2.31 us
    pallas_call x1, Pallas kernels, shards(): call(stats_kernel, in_specs=[HBM] * 6, out_specs=[VMEM] * 7, out_shape=[s...  1.85 us

profile of v3, /device:TPU:16, one launch (start us, length us, event | category | flops | bytes accessed | tf_op | source)
XLA Modules:
  0.0 80.9 jit_solution(11748453364180290783)
XLA Ops:
  0.6 1.9 %stats.1 = (f32[16,8,128]{2,1,0:T(8,128)S(1)}, bf16[512,384]{1,0:T(8,128)(2,1)S(1)}, bf16[512,384]{1,0:T(8,128)(2,1)S(1)}, f32[384]{0:T(512)S(1)}, bf16[512,384]...) custom-call(bf16[512,384]{1,0:T(8,128)(2,1)} %out_hbm.1, bf16[512,384]{1,0:T(8,128)(2,1)} %grad_hbm.1, ...), custom_call_target="tpu_custom_call" | custom-call | tf_op jit(solution)/shard_map/stats/pallas_call | solution.py:206
  2.5 14.5 %all_to_all.15.parts_ref = f32[16,8,128]{2,1,0:T(8,128)S(1)} all-to-all(f32[16,8,128]{2,1,0:T(8,128)S(1)} %get-tuple-element.15), channel_id=1, replica_groups=mesh['seq'=64,'head'=16] {'head'}, dimensions={0} | all-to-all | bytes 131072 | tf_op jit(solution)/shard_map/all_to_all | solution.py:224
  17.0 2.3 %grad_out.1 = (bf16[512,384]{1,0:T(8,128)(2,1)S(1)}, f32[768,128]{1,0:T(8,128)S(1)}, f32[384,128]{1,0:T(8,128)S(1)}, f32[384,128]{1,0:T(8,128)S(1)}, f32[3,512,384]{2,1,0:T(8,128)S(1)}) custom-call(f32[16,8,128]{2,1,0:T(8,128)S(1)} %all_to_all.15.parts_ref, bf16[512,384]{1,0:T(8,128)(2,1)S(1)} %get-tuple-element.16.out_ref, ...), custom_call_target="tpu_custom_call" | custom-call | tf_op jit(solution)/shard_map/grad_out/pallas_call | solution.py:225
  19.3 38.7 %all_to_all.16 = f32[64,1,1536]{2,1,0:T(1,128)S(1)} all-to-all(f32[64,1,1536]{2,1,0:T(1,128)S(1)} %bitcast.7), channel_id=1, replica_groups=mesh['seq'=64,'head'=16] {'seq'}, dimensions={0} | all-to-all | bytes 786432 | tf_op jit(solution)/shard_map/all_to_all | solution.py:239
  58.1 0.1 scan.1
  58.2 21.4 %all_to_all.17 = f32[64,1,1536]{2,1,0:T(1,128)S(1)} all-to-all(f32[64,1,1536]{2,1,0:T(1,128)S(1)} %bitcast.6), channel_id=1, replica_groups=mesh['seq'=64,'head'=16] {'seq'}, dimensions={0} | all-to-all | bytes 786432 | tf_op jit(solution)/shard_map/all_to_all | solution.py:247
  79.5 1.4 %outputs.1 = (bf16[512,384]{1,0:T(8,128)(2,1)}, bf16[512,384]{1,0:T(8,128)(2,1)}, bf16[512,384]{1,0:T(8,128)(2,1)}) custom-call(f32[768,128]{1,0:T(8,128)S(1)} %bitcast.4, f32[384,128]{1,0:T(8,128)S(1)} %get-tuple-element.23.kv0_ref, f32[384,128]{1,0:T(8,128)S(1)} %get-tuple-element.24.qg1_ref, bf16[512,384]{1,0:T(8,128)(2,1)S(1)} %get-tuple-element.19.q_ref, ...), custom_call_target="tpu_custom_call" | custom-call | tf_op jit(solution)/shard_map/outputs/pallas_call | solution.py:248

commit v4 on v3

--- a/solution.py
+++ b/solution.py
@@ -24,6 +24,18 @@
 NN = ((1,), (0,))
 NT = ((1,), (1,))
 TN = ((0,), (0,))
+
+
+def ring(count):
+    return math.isqrt(count)
+
+
+def segments(first, rows, step):
+    at = first
+    while at < first + rows:
+        end = min(first + rows, (at // step + 1) * step)
+        yield at // step, at % step, at - first, end - at
+        at = end
 
 
 def early():
@@ -102,7 +114,11 @@
         o = out_ref[here, :].astype(F32)
         g = s * columns[:, r : r + 1] - o * columns[:, rows + r : rows + r + 1]
         g_ref[here, :] = g.astype(BF16)
-    half = heads * DH
+    step = state_ref.shape[1] // 2
+
+    def put(value, h, offset):
+        for piece, to, at, length in segments(h * DH, DH, step):
+            state_ref[piece, offset + to : offset + to + length, :] = value[at : at + length]
 
     def terms(a_ref, b_ref, h):
         cols = pl.ds(h * DH, DH)
@@ -111,11 +127,11 @@
     for h in range(heads):
         qg = terms(q_ref, g_ref, h)
         qg1_ref[pl.ds(h * DH, DH), :] = qg[1]
-        state_ref[pl.ds(half + h * DH, DH), :] = qg[0] + qg[1]
+        put(qg[0] + qg[1], h, step)
     for h in range(heads):
         kv = terms(k_ref, v_ref, h)
         kv0_ref[pl.ds(h * DH, DH), :] = kv[0]
-        state_ref[pl.ds(h * DH, DH), :] = kv[0] + kv[1]
+        put(kv[0] + kv[1], h, 0)
 
 
     @pl.when(early())
@@ -128,30 +144,41 @@
                     inner_ref[i, here, cols] = value
 
 
-def scan_kernel(count, x_ref, y_ref):
-    step = x_ref.shape[0] // count
-    forward = lax.axis_index("seq") < count // 2
-
-    def scan(order):
-        total = jnp.zeros((step, x_ref.shape[1]), F32)
-        for p in order:
-            y_ref[p * step : (p + 1) * step, :] = total
-            total = total + x_ref[p * step : (p + 1) * step, :]
-
-    @pl.when(forward)
-    def _():
-        scan(range(count))
-
-    @pl.when(jnp.logical_not(forward))
-    def _():
-        scan(range(count - 1, -1, -1))
+def totals_kernel(x_ref, send_ref):
+    count, both, _ = x_ref.shape
+    step = both // 2
+    z = lax.axis_index("seq") // count
+    kv = x_ref[0, :step, :]
+    qg = x_ref[0, step:, :]
+    for y in range(1, count):
+        kv = kv + x_ref[y, :step, :]
+        qg = qg + x_ref[y, step:, :]
+    for other in range(send_ref.shape[0]):
+        send_ref[other] = jnp.where(other > z, kv, qg)
+
+
+def sums_kernel(x_ref, rows_ref, y_ref):
+    count, both, _ = x_ref.shape
+    step = both // 2
+    z = lax.axis_index("seq") // count
+    zeros = jnp.zeros((step, x_ref.shape[2]), F32)
+    kv, qg = zeros, zeros
+    for other in range(rows_ref.shape[0]):
+        kv = kv + jnp.where(other < z, rows_ref[other], zeros)
+        qg = qg + jnp.where(other > z, rows_ref[other], zeros)
+    for y in range(count):
+        y_ref[y, :step, :] = kv
+        kv = kv + x_ref[y, :step, :]
+    for y in range(count - 1, -1, -1):
+        y_ref[y, step:, :] = qg
+        qg = qg + x_ref[y, step:, :]
 
 
 def output_kernel(factor, carry_ref, kv0_ref, qg1_ref, q_ref, k_ref, v_ref, g_ref, inner_ref,
                   qgrad_hbm, kgrad_hbm, vgrad_hbm, qgrad_ref, kgrad_ref, vgrad_ref, sems):
     width = q_ref.shape[1]
     heads = width // DH
-    half = heads * DH
+    step = carry_ref.shape[1] // 2
     results = ((qgrad_ref, qgrad_hbm), (kgrad_ref, kgrad_hbm), (vgrad_ref, vgrad_hbm))
 
     def copy_of(i, b, h):
@@ -159,11 +186,17 @@
         ref, hbm = results[i]
         return pltpu.make_async_copy(ref.at[here, cols], hbm.at[here, cols], sems.at[i, b, h])
 
+    def state(h, offset):
+        runs = [
+            carry_ref[piece, offset + to : offset + to + length, :]
+            for piece, to, _, length in segments(h * DH, DH, step)
+        ]
+        return jnp.concatenate(runs, axis=0)
+
     def finish(inner):
         for h in range(heads):
             cols = pl.ds(h * DH, DH)
-            before = carry_ref[pl.ds(h * DH, DH), :]
-            after = carry_ref[pl.ds(half + h * DH, DH), :]
+            before, after = state(h, 0), state(h, step)
             for b in range(2):
                 here = pl.ds(b * GROUP, GROUP)
                 q, k, v, g = q_ref[here, cols], k_ref[here, cols], v_ref[here, cols], g_ref[here, cols]
@@ -200,6 +233,10 @@
     full_width = width * n_head
     factor = 1.0 / math.sqrt(DH * tokens * n_seq)
     shape = jax.ShapeDtypeStruct
+    n_ring = ring(n_seq)
+    rows = [[z * n_ring + y for y in range(n_ring)] for z in range(n_seq // n_ring)]
+    columns = [list(column) for column in zip(*rows)]
+    exchanged = (n_ring, 2 * width // n_ring, DH)
     far = functools.partial(pltpu.with_memory_space_constraint, memory_space=pltpu.HBM)
     params = pltpu.CompilerParams(vmem_limit_bytes=16 << 20)
     call = functools.partial(pl.pallas_call, compiler_params=params)
@@ -228,23 +265,30 @@
         out_specs=[VMEM] * 5,
         out_shape=[
             shape((tokens, width), BF16),
-            shape((2 * width, DH), F32),
+            shape(exchanged, F32),
             shape((width, DH), F32),
             shape((width, DH), F32),
             shape((3, tokens, width), F32),
         ],
         name="grad_out",
     )(parts, out_near, grad_near, gain_near, *near)
-    piece = 2 * width * DH // n_seq
-    gathered = lax.all_to_all(state.reshape(n_seq, 1, piece), "seq", 0, 0)
-    scanned = call(
-        functools.partial(scan_kernel, n_seq),
+    gathered = lax.all_to_all(state, "seq", 0, 0, axis_index_groups=rows)
+    totals = call(
+        totals_kernel,
         in_specs=[VMEM],
         out_specs=VMEM,
-        out_shape=shape((2 * width, DH), F32),
-        name="scan",
-    )(gathered.reshape(2 * width, DH))
-    carry = lax.all_to_all(scanned.reshape(n_seq, 1, piece), "seq", 0, 0)
+        out_shape=shape((n_seq // n_ring, width // n_ring, DH), F32),
+        name="totals",
+    )(gathered)
+    others = lax.all_to_all(totals, "seq", 0, 0, axis_index_groups=columns)
+    sums = call(
+        sums_kernel,
+        in_specs=[VMEM] * 2,
+        out_specs=VMEM,
+        out_shape=shape(exchanged, F32),
+        name="sums",
+    )(gathered, others)
+    carry = lax.all_to_all(sums, "seq", 0, 0, axis_index_groups=rows)
     return call(
         functools.partial(output_kernel, factor),
         in_specs=[VMEM] * 8,
@@ -253,7 +297,7 @@
         scratch_shapes=[pltpu.VMEM((tokens, width), BF16)] * 3
         + [pltpu.SemaphoreType.DMA((3, tokens // GROUP, width // DH))],
         name="outputs",
-    )(carry.reshape(2 * width, DH), kv0, qg1, *near, g, inner)
+    )(carry, kv0, qg1, *near, g, inner)
 
 
 def solution(mesh):

time: 81.1 us -> 83.2 us (1.026)
  blocking collectives: 74.6 us -> 76.7 us
    all_to_all x2 -> x3, blocking collectives: 60.1 us -> 62.2 us  [the longest x1 25.3 us: shards(): gathered = lax.all_to_all(state, 'seq', 0, 0, axis_index_groups=rows)]
where the time goes in v4:
time: 83.2 us; the launch traced here: 83 us
  blocking collectives  76.7 us (92%)
  Pallas kernels  5.62 us (7%)
    all_to_all x1, blocking collectives, shards(): gathered = lax.all_to_all(state, 'seq', 0, 0, axis_index_groups=rows)  25.3 us
    all_to_all x1, blocking collectives, shards(): others = lax.all_to_all(totals, 'seq', 0, 0, axis_index_groups=columns)  20.9 us
    all_to_all x1, blocking collectives, shards(): carry = lax.all_to_all(sums, 'seq', 0, 0, axis_index_groups=rows)  16 us
    all_to_all x1, blocking collectives, shards(): parts = lax.all_to_all(send, 'head', 0, 0)  14.5 us
    pallas_call x1, Pallas kernels, shards(): call(functools.partial(grad_out_kernel, full_width), in_specs=[VMEM] * 7,...  2.31 us
    pallas_call x1, Pallas kernels, shards(): call(stats_kernel, in_specs=[HBM] * 6, out_specs=[VMEM] * 7, out_shape=[s...  1.85 us

profile of v4, /device:TPU:16, one launch (start us, length us, event | category | flops | bytes accessed | tf_op | source)
XLA Modules:
  0.0 83.0 jit_solution(916137224616548298)
XLA Ops:
  0.6 1.9 %stats.1 = (f32[16,8,128]{2,1,0:T(8,128)S(1)}, bf16[512,384]{1,0:T(8,128)(2,1)S(1)}, bf16[512,384]{1,0:T(8,128)(2,1)S(1)}, f32[384]{0:T(512)S(1)}, bf16[512,384]...) custom-call(bf16[512,384]{1,0:T(8,128)(2,1)} %out_hbm.1, bf16[512,384]{1,0:T(8,128)(2,1)} %grad_hbm.1, ...), custom_call_target="tpu_custom_call" | custom-call | tf_op jit(solution)/shard_map/stats/pallas_call | solution.py:243
  2.5 14.5 %all_to_all.20.parts_ref = f32[16,8,128]{2,1,0:T(8,128)S(1)} all-to-all(f32[16,8,128]{2,1,0:T(8,128)S(1)} %get-tuple-element.15), channel_id=1, replica_groups=mesh['seq'=64,'head'=16] {'head'}, dimensions={0} | all-to-all | bytes 131072 | tf_op jit(solution)/shard_map/all_to_all | solution.py:261
  17.0 2.3 %grad_out.1 = (bf16[512,384]{1,0:T(8,128)(2,1)S(1)}, f32[8,96,128]{2,1,0:T(8,128)S(1)}, f32[384,128]{1,0:T(8,128)S(1)}, f32[384,128]{1,0:T(8,128)S(1)}, f32[3,512,384]{2,1,0:T(8,128)S(1)}) custom-call(f32[16,8,128]{2,1,0:T(8,128)S(1)} %all_to_all.20.parts_ref, bf16[512,384]{1,0:T(8,128)(2,1)S(1)} %get-tuple-element.16.out_ref, ...), custom_call_target="tpu_custom_call" | custom-call | tf_op jit(solution)/shard_map/grad_out/pallas_call | solution.py:262
  19.3 25.3 %all_to_all.21.x_ref = f32[8,96,128]{2,1,0:T(8,128)S(1)} all-to-all(f32[8,96,128]{2,1,0:T(8,128)S(1)} %get-tuple-element.22), channel_id=1, replica_groups={{0,16,32,48,64,80,96,112},{128,144,160,176,192,208,224,240},{256,272,28..., dimensions={0} | all-to-all | bytes 786432 | tf_op jit(solution)/shard_map/all_to_all | solution.py:275
  44.6 20.9 %all_to_all.22.rows_ref = f32[8,48,128]{2,1,0:T(8,128)S(1)} all-to-all(f32[8,48,128]{2,1,0:T(8,128)S(1)} %totals.1), channel_id=1, replica_groups={{0,128,256,384,512,640,768,896},{16,144,272,400,528,656,784,912},{32,16..., dimensions={0} | all-to-all | bytes 393216 | tf_op jit(solution)/shard_map/all_to_all | solution.py:283
  65.5 0.1 sums.1
  65.6 16.0 %all_to_all.23.carry_ref = f32[8,96,128]{2,1,0:T(8,128)S(1)} all-to-all(f32[8,96,128]{2,1,0:T(8,128)S(1)} %sums.1), channel_id=1, replica_groups={{0,16,32,48,64,80,96,112},{128,144,160,176,192,208,224,240},{256,272,28..., dimensions={0} | all-to-all | bytes 786432 | tf_op jit(solution)/shard_map/all_to_all | solution.py:291
  81.6 1.4 %outputs.1 = (bf16[512,384]{1,0:T(8,128)(2,1)}, bf16[512,384]{1,0:T(8,128)(2,1)}, bf16[512,384]{1,0:T(8,128)(2,1)}) custom-call(f32[8,96,128]{2,1,0:T(8,128)S(1)} %all_to_all.23.carry_ref, f32[384,128]{1,0:T(8,128)S(1)} %get-tuple-element.23.kv0_ref, f32[384,128]{1,0:T(8,128)S(1)} %get-tuple-element.24.qg1_ref, ...), custom_call_target="tpu_custom_call" | custom-call | tf_op jit(solution)/shard_map/outputs/pallas_call | solution.py:292
  (1 shorter events, 0.0 us)

commit v5 on v3

--- a/solution.py
+++ b/solution.py
@@ -27,7 +27,8 @@
 
 
 def early():
-    return lax.axis_index("seq") * 8 < lax.axis_size("seq") * 5
+    waits = lax.axis_index("seq") * 8 < lax.axis_size("seq") * 5
+    return jnp.logical_or(waits, lax.rem(lax.axis_index("head"), 2) == 1)
 
 
 def within_block(q, k, v, g):

time: 81.1 us -> 82.3 us (1.015)
  blocking collectives: 74.6 us -> 75.8 us
    all_to_all x1, blocking collectives: 21.4 us -> 22.8 us  [shards(): carry = lax.all_to_all(scanned.reshape(n_seq, 1, piece), 'seq', 0, 0)]
where the time goes in v5:
time: 82.3 us; the launch traced here: 82.1 us
  blocking collectives  75.8 us (92%)
  Pallas kernels  5.6 us (7%)
    all_to_all x1, blocking collectives, shards(): gathered = lax.all_to_all(state.reshape(n_seq, 1, piece), 'seq', 0, 0)  38.5 us
    all_to_all x1, blocking collectives, shards(): carry = lax.all_to_all(scanned.reshape(n_seq, 1, piece), 'seq', 0, 0)  22.8 us
    all_to_all x1, blocking collectives, shards(): parts = lax.all_to_all(send, 'head', 0, 0)  14.5 us
    pallas_call x1, Pallas kernels, shards(): call(functools.partial(grad_out_kernel, full_width), in_specs=[VMEM] * 7,...  2.31 us
    pallas_call x1, Pallas kernels, shards(): call(stats_kernel, in_specs=[HBM] * 6, out_specs=[VMEM] * 7, out_shape=[s...  1.85 us

profile of v5, /device:TPU:16, one launch (start us, length us, event | category | flops | bytes accessed | tf_op | source)
XLA Modules:
  0.0 82.1 jit_solution(5336986556287225149)
XLA Ops:
  0.6 1.9 %stats.1 = (f32[16,8,128]{2,1,0:T(8,128)S(1)}, bf16[512,384]{1,0:T(8,128)(2,1)S(1)}, bf16[512,384]{1,0:T(8,128)(2,1)S(1)}, f32[384]{0:T(512)S(1)}, bf16[512,384]...) custom-call(bf16[512,384]{1,0:T(8,128)(2,1)} %out_hbm.1, bf16[512,384]{1,0:T(8,128)(2,1)} %grad_hbm.1, ...), custom_call_target="tpu_custom_call" | custom-call | tf_op jit(solution)/shard_map/stats/pallas_call | solution.py:207
  2.5 14.5 %all_to_all.15.parts_ref = f32[16,8,128]{2,1,0:T(8,128)S(1)} all-to-all(f32[16,8,128]{2,1,0:T(8,128)S(1)} %get-tuple-element.15), channel_id=1, replica_groups=mesh['seq'=64,'head'=16] {'head'}, dimensions={0} | all-to-all | bytes 131072 | tf_op jit(solution)/shard_map/all_to_all | solution.py:225
  17.0 2.3 %grad_out.1 = (bf16[512,384]{1,0:T(8,128)(2,1)S(1)}, f32[768,128]{1,0:T(8,128)S(1)}, f32[384,128]{1,0:T(8,128)S(1)}, f32[384,128]{1,0:T(8,128)S(1)}, f32[3,512,384]{2,1,0:T(8,128)S(1)}) custom-call(f32[16,8,128]{2,1,0:T(8,128)S(1)} %all_to_all.15.parts_ref, bf16[512,384]{1,0:T(8,128)(2,1)S(1)} %get-tuple-element.16.out_ref, ...), custom_call_target="tpu_custom_call" | custom-call | tf_op jit(solution)/shard_map/grad_out/pallas_call | solution.py:226
  19.3 38.5 %all_to_all.16 = f32[64,1,1536]{2,1,0:T(1,128)S(1)} all-to-all(f32[64,1,1536]{2,1,0:T(1,128)S(1)} %bitcast.7), channel_id=1, replica_groups=mesh['seq'=64,'head'=16] {'seq'}, dimensions={0} | all-to-all | bytes 786432 | tf_op jit(solution)/shard_map/all_to_all | solution.py:240
  57.9 0.1 scan.1
  57.9 22.8 %all_to_all.17 = f32[64,1,1536]{2,1,0:T(1,128)S(1)} all-to-all(f32[64,1,1536]{2,1,0:T(1,128)S(1)} %bitcast.6), channel_id=1, replica_groups=mesh['seq'=64,'head'=16] {'seq'}, dimensions={0} | all-to-all | bytes 786432 | tf_op jit(solution)/shard_map/all_to_all | solution.py:248
  80.7 1.4 %outputs.1 = (bf16[512,384]{1,0:T(8,128)(2,1)}, bf16[512,384]{1,0:T(8,128)(2,1)}, bf16[512,384]{1,0:T(8,128)(2,1)}) custom-call(f32[768,128]{1,0:T(8,128)S(1)} %bitcast.4, f32[384,128]{1,0:T(8,128)S(1)} %get-tuple-element.23.kv0_ref, f32[384,128]{1,0:T(8,128)S(1)} %get-tuple-element.24.qg1_ref, bf16[512,384]{1,0:T(8,128)(2,1)S(1)} %get-tuple-element.19.q_ref, ...), custom_call_target="tpu_custom_call" | custom-call | tf_op jit(solution)/shard_map/outputs/pallas_call | solution.py:249

commit v6 on v3

--- a/solution.py
+++ b/solution.py
@@ -40,34 +40,26 @@
 
 
 def stats_kernel(out_hbm, grad_hbm, gain_hbm, q_hbm, k_hbm, v_hbm,
-                 send_ref, out_ref, grad_ref, gain_ref, q_ref, k_ref, v_ref, sems, gain_sem, later_sems):
+                 send_ref, out_ref, grad_ref, gain_ref, q_ref, k_ref, v_ref, sems):
     tokens, width = out_ref.shape
     rows = tokens // DH
-    copies = []
-    for r in range(rows):
-        here = pl.ds(r * DH, DH)
-        copies.append(
-            (
-                pltpu.make_async_copy(out_hbm.at[here], out_ref.at[here], sems.at[0, r]),
-                pltpu.make_async_copy(grad_hbm.at[here], grad_ref.at[here], sems.at[1, r]),
-            )
-        )
-    gain_copy = pltpu.make_async_copy(gain_hbm, gain_ref, gain_sem)
+    first = [
+        pltpu.make_async_copy(out_hbm, out_ref, sems.at[0]),
+        pltpu.make_async_copy(grad_hbm, grad_ref, sems.at[1]),
+    ]
+    first.append(pltpu.make_async_copy(gain_hbm, gain_ref, sems.at[2]))
     later = [
-        pltpu.make_async_copy(hbm, ref, later_sems.at[i])
+        pltpu.make_async_copy(hbm, ref, sems.at[3 + i])
         for i, (hbm, ref) in enumerate(((q_hbm, q_ref), (k_hbm, k_ref), (v_hbm, v_ref)))
     ]
-    gain_copy.start()
-    for pair in copies:
-        pair[0].start()
-        pair[1].start()
+    for copy in first:
+        copy.start()
     for copy in later:
-        copy.start()
-    gain_copy.wait()
+        copy.start(priority=1)
+    for copy in first:
+        copy.wait()
     gain = gain_ref[...].reshape(1, width)
     for r in range(rows):
-        copies[r][0].wait()
-        copies[r][1].wait()
         o = out_ref[pl.ds(r * DH, DH), :].astype(F32)
         s = grad_ref[pl.ds(r * DH, DH), :].astype(F32) * gain
         oo, so = o * o, s * o
@@ -89,9 +81,10 @@
     tokens, width = out_ref.shape
     heads = width // DH
     rows = tokens // DH
-    total = parts_ref[0]
-    for d in range(1, parts_ref.shape[0]):
-        total = total + parts_ref[d]
+    parts = [parts_ref[d] for d in range(parts_ref.shape[0])]
+    while len(parts) > 1:
+        parts = [a + b for a, b in zip(parts[::2], parts[1::2])]
+    total = parts[0]
     inv = lax.rsqrt(total[:rows] / full_width + EPS)
     coef = total[rows:] * (inv * inv * inv) / full_width
     columns = jnp.concatenate([inv, coef], axis=0).T
@@ -214,11 +207,7 @@
             shape((width,), F32),
         ]
         + [shape((tokens, width), BF16)] * 3,
-        scratch_shapes=[
-            pltpu.SemaphoreType.DMA((2, tokens // DH)),
-            pltpu.SemaphoreType.DMA,
-            pltpu.SemaphoreType.DMA((3,)),
-        ],
+        scratch_shapes=[pltpu.SemaphoreType.DMA((6,))],
         name="stats",
     )(*map(far, (attn_out, out_grad, norm_gain, queries, keys, values)))
     parts = lax.all_to_all(send, "head", 0, 0)

time: 81.1 us -> 80.8 us (level)
  no operation moved by 1% of the time
where the time goes in v6:
time: 80.8 us; the launch traced here: 80.6 us
  blocking collectives  74.6 us (92%)
  Pallas kernels  5.27 us (7%)
    all_to_all x1, blocking collectives, shards(): gathered = lax.all_to_all(state.reshape(n_seq, 1, piece), 'seq', 0, 0)  38.7 us
    all_to_all x1, blocking collectives, shards(): carry = lax.all_to_all(scanned.reshape(n_seq, 1, piece), 'seq', 0, 0)  21.4 us
    all_to_all x1, blocking collectives, shards(): parts = lax.all_to_all(send, 'head', 0, 0)  14.5 us
    pallas_call x1, Pallas kernels, shards(): call(functools.partial(grad_out_kernel, full_width), in_specs=[VMEM] * 7,...  2.3 us

profile of v6, /device:TPU:16, one launch (start us, length us, event | category | flops | bytes accessed | tf_op | source)
XLA Modules:
  0.0 80.6 jit_solution(3018687166295751346)
XLA Ops:
  0.6 1.5 %stats.1 = (f32[16,8,128]{2,1,0:T(8,128)S(1)}, bf16[512,384]{1,0:T(8,128)(2,1)S(1)}, bf16[512,384]{1,0:T(8,128)(2,1)S(1)}, f32[384]{0:T(512)S(1)}, bf16[512,384]...) custom-call(bf16[512,384]{1,0:T(8,128)(2,1)} %out_hbm.1, bf16[512,384]{1,0:T(8,128)(2,1)} %grad_hbm.1, ...), custom_call_target="tpu_custom_call" | custom-call | tf_op jit(solution)/shard_map/stats/pallas_call | solution.py:199
  2.2 14.5 %all_to_all.15.parts_ref = f32[16,8,128]{2,1,0:T(8,128)S(1)} all-to-all(f32[16,8,128]{2,1,0:T(8,128)S(1)} %get-tuple-element.15), channel_id=1, replica_groups=mesh['seq'=64,'head'=16] {'head'}, dimensions={0} | all-to-all | bytes 131072 | tf_op jit(solution)/shard_map/all_to_all | solution.py:213
  16.7 2.3 %grad_out.1 = (bf16[512,384]{1,0:T(8,128)(2,1)S(1)}, f32[768,128]{1,0:T(8,128)S(1)}, f32[384,128]{1,0:T(8,128)S(1)}, f32[384,128]{1,0:T(8,128)S(1)}, f32[3,512,384]{2,1,0:T(8,128)S(1)}) custom-call(f32[16,8,128]{2,1,0:T(8,128)S(1)} %all_to_all.15.parts_ref, bf16[512,384]{1,0:T(8,128)(2,1)S(1)} %get-tuple-element.16.out_ref, ...), custom_call_target="tpu_custom_call" | custom-call | tf_op jit(solution)/shard_map/grad_out/pallas_call | solution.py:214
  19.0 38.7 %all_to_all.16 = f32[64,1,1536]{2,1,0:T(1,128)S(1)} all-to-all(f32[64,1,1536]{2,1,0:T(1,128)S(1)} %bitcast.7), channel_id=1, replica_groups=mesh['seq'=64,'head'=16] {'seq'}, dimensions={0} | all-to-all | bytes 786432 | tf_op jit(solution)/shard_map/all_to_all | solution.py:228
  57.8 0.1 scan.1
  57.8 21.4 %all_to_all.17 = f32[64,1,1536]{2,1,0:T(1,128)S(1)} all-to-all(f32[64,1,1536]{2,1,0:T(1,128)S(1)} %bitcast.6), channel_id=1, replica_groups=mesh['seq'=64,'head'=16] {'seq'}, dimensions={0} | all-to-all | bytes 786432 | tf_op jit(solution)/shard_map/all_to_all | solution.py:236
  79.2 1.4 %outputs.1 = (bf16[512,384]{1,0:T(8,128)(2,1)}, bf16[512,384]{1,0:T(8,128)(2,1)}, bf16[512,384]{1,0:T(8,128)(2,1)}) custom-call(f32[768,128]{1,0:T(8,128)S(1)} %bitcast.4, f32[384,128]{1,0:T(8,128)S(1)} %get-tuple-element.23.kv0_ref, f32[384,128]{1,0:T(8,128)S(1)} %get-tuple-element.24.qg1_ref, bf16[512,384]{1,0:T(8,128)(2,1)S(1)} %get-tuple-element.19.q_ref, ...), custom_call_target="tpu_custom_call" | custom-call | tf_op jit(solution)/shard_map/outputs/pallas_call | solution.py:237

commit v7 on v6

--- a/solution.py
+++ b/solution.py
@@ -27,7 +27,8 @@
 
 
 def early():
-    return lax.axis_index("seq") * 8 < lax.axis_size("seq") * 5
+    waits = lax.axis_index("seq") * 8 < lax.axis_size("seq") * 5
+    return jnp.logical_or(waits, lax.rem(lax.axis_index("head"), 2) == 0)
 
 
 def within_block(q, k, v, g):

time: 80.8 us -> 80.2 us (level)
    all_to_all x1, blocking collectives: 21.4 us -> 20.5 us  [shards(): carry = lax.all_to_all(scanned.reshape(n_seq, 1, piece), 'seq', 0, 0)]
where the time goes in v7:
time: 80.2 us; the launch traced here: 80 us
  blocking collectives  74.1 us (92%)
  Pallas kernels  5.28 us (7%)
    all_to_all x1, blocking collectives, shards(): gathered = lax.all_to_all(state.reshape(n_seq, 1, piece), 'seq', 0, 0)  39 us
    all_to_all x1, blocking collectives, shards(): carry = lax.all_to_all(scanned.reshape(n_seq, 1, piece), 'seq', 0, 0)  20.5 us
    all_to_all x1, blocking collectives, shards(): parts = lax.all_to_all(send, 'head', 0, 0)  14.5 us
    pallas_call x1, Pallas kernels, shards(): call(functools.partial(grad_out_kernel, full_width), in_specs=[VMEM] * 7,...  2.3 us

profile of v7, /device:TPU:16, one launch (start us, length us, event | category | flops | bytes accessed | tf_op | source)
XLA Modules:
  0.0 80.0 jit_solution(156215303033311201)
XLA Ops:
  0.6 1.5 %stats.1 = (f32[16,8,128]{2,1,0:T(8,128)S(1)}, bf16[512,384]{1,0:T(8,128)(2,1)S(1)}, bf16[512,384]{1,0:T(8,128)(2,1)S(1)}, f32[384]{0:T(512)S(1)}, bf16[512,384]...) custom-call(bf16[512,384]{1,0:T(8,128)(2,1)} %out_hbm.1, bf16[512,384]{1,0:T(8,128)(2,1)} %grad_hbm.1, ...), custom_call_target="tpu_custom_call" | custom-call | tf_op jit(solution)/shard_map/stats/pallas_call | solution.py:200
  2.2 14.5 %all_to_all.15.parts_ref = f32[16,8,128]{2,1,0:T(8,128)S(1)} all-to-all(f32[16,8,128]{2,1,0:T(8,128)S(1)} %get-tuple-element.15), channel_id=1, replica_groups=mesh['seq'=64,'head'=16] {'head'}, dimensions={0} | all-to-all | bytes 131072 | tf_op jit(solution)/shard_map/all_to_all | solution.py:214
  16.7 2.3 %grad_out.1 = (bf16[512,384]{1,0:T(8,128)(2,1)S(1)}, f32[768,128]{1,0:T(8,128)S(1)}, f32[384,128]{1,0:T(8,128)S(1)}, f32[384,128]{1,0:T(8,128)S(1)}, f32[3,512,384]{2,1,0:T(8,128)S(1)}) custom-call(f32[16,8,128]{2,1,0:T(8,128)S(1)} %all_to_all.15.parts_ref, bf16[512,384]{1,0:T(8,128)(2,1)S(1)} %get-tuple-element.16.out_ref, ...), custom_call_target="tpu_custom_call" | custom-call | tf_op jit(solution)/shard_map/grad_out/pallas_call | solution.py:215
  19.0 39.0 %all_to_all.16 = f32[64,1,1536]{2,1,0:T(1,128)S(1)} all-to-all(f32[64,1,1536]{2,1,0:T(1,128)S(1)} %bitcast.7), channel_id=1, replica_groups=mesh['seq'=64,'head'=16] {'seq'}, dimensions={0} | all-to-all | bytes 786432 | tf_op jit(solution)/shard_map/all_to_all | solution.py:229
  58.0 0.1 scan.1
  58.1 20.5 %all_to_all.17 = f32[64,1,1536]{2,1,0:T(1,128)S(1)} all-to-all(f32[64,1,1536]{2,1,0:T(1,128)S(1)} %bitcast.6), channel_id=1, replica_groups=mesh['seq'=64,'head'=16] {'seq'}, dimensions={0} | all-to-all | bytes 786432 | tf_op jit(solution)/shard_map/all_to_all | solution.py:237
  78.6 1.4 %outputs.1 = (bf16[512,384]{1,0:T(8,128)(2,1)}, bf16[512,384]{1,0:T(8,128)(2,1)}, bf16[512,384]{1,0:T(8,128)(2,1)}) custom-call(f32[768,128]{1,0:T(8,128)S(1)} %bitcast.4, f32[384,128]{1,0:T(8,128)S(1)} %get-tuple-element.23.kv0_ref, f32[384,128]{1,0:T(8,128)S(1)} %get-tuple-element.24.qg1_ref, bf16[512,384]{1,0:T(8,128)(2,1)S(1)} %get-tuple-element.19.q_ref, ...), custom_call_target="tpu_custom_call" | custom-call | tf_op jit(solution)/shard_map/outputs/pallas_call | solution.py:238

commit v8 on v4

--- a/solution.py
+++ b/solution.py
@@ -39,7 +39,8 @@
 
 
 def early():
-    return lax.axis_index("seq") * 8 < lax.axis_size("seq") * 5
+    waits = lax.axis_index("seq") * 8 < lax.axis_size("seq") * 5
+    return jnp.logical_or(waits, lax.rem(lax.axis_index("head"), 2) == 0)
 
 
 def within_block(q, k, v, g):
@@ -52,34 +53,26 @@
 
 
 def stats_kernel(out_hbm, grad_hbm, gain_hbm, q_hbm, k_hbm, v_hbm,
-                 send_ref, out_ref, grad_ref, gain_ref, q_ref, k_ref, v_ref, sems, gain_sem, later_sems):
+                 send_ref, out_ref, grad_ref, gain_ref, q_ref, k_ref, v_ref, sems):
     tokens, width = out_ref.shape
     rows = tokens // DH
-    copies = []
-    for r in range(rows):
-        here = pl.ds(r * DH, DH)
-        copies.append(
-            (
-                pltpu.make_async_copy(out_hbm.at[here], out_ref.at[here], sems.at[0, r]),
-                pltpu.make_async_copy(grad_hbm.at[here], grad_ref.at[here], sems.at[1, r]),
-            )
-        )
-    gain_copy = pltpu.make_async_copy(gain_hbm, gain_ref, gain_sem)
+    first = [
+        pltpu.make_async_copy(out_hbm, out_ref, sems.at[0]),
+        pltpu.make_async_copy(grad_hbm, grad_ref, sems.at[1]),
+    ]
+    first.append(pltpu.make_async_copy(gain_hbm, gain_ref, sems.at[2]))
     later = [
-        pltpu.make_async_copy(hbm, ref, later_sems.at[i])
+        pltpu.make_async_copy(hbm, ref, sems.at[3 + i])
         for i, (hbm, ref) in enumerate(((q_hbm, q_ref), (k_hbm, k_ref), (v_hbm, v_ref)))
     ]
-    gain_copy.start()
-    for pair in copies:
-        pair[0].start()
-        pair[1].start()
+    for copy in first:
+        copy.start()
     for copy in later:
-        copy.start()
-    gain_copy.wait()
+        copy.start(priority=1)
+    for copy in first:
+        copy.wait()
     gain = gain_ref[...].reshape(1, width)
     for r in range(rows):
-        copies[r][0].wait()
-        copies[r][1].wait()
         o = out_ref[pl.ds(r * DH, DH), :].astype(F32)
         s = grad_ref[pl.ds(r * DH, DH), :].astype(F32) * gain
         oo, so = o * o, s * o
@@ -101,9 +94,10 @@
     tokens, width = out_ref.shape
     heads = width // DH
     rows = tokens // DH
-    total = parts_ref[0]
-    for d in range(1, parts_ref.shape[0]):
-        total = total + parts_ref[d]
+    parts = [parts_ref[d] for d in range(parts_ref.shape[0])]
+    while len(parts) > 1:
+        parts = [a + b for a, b in zip(parts[::2], parts[1::2])]
+    total = parts[0]
     inv = lax.rsqrt(total[:rows] / full_width + EPS)
     coef = total[rows:] * (inv * inv * inv) / full_width
     columns = jnp.concatenate([inv, coef], axis=0).T
@@ -251,11 +245,7 @@
             shape((width,), F32),
         ]
         + [shape((tokens, width), BF16)] * 3,
-        scratch_shapes=[
-            pltpu.SemaphoreType.DMA((2, tokens // DH)),
-            pltpu.SemaphoreType.DMA,
-            pltpu.SemaphoreType.DMA((3,)),
-        ],
+        scratch_shapes=[pltpu.SemaphoreType.DMA((6,))],
         name="stats",
     )(*map(far, (attn_out, out_grad, norm_gain, queries, keys, values)))
     parts = lax.all_to_all(send, "head", 0, 0)

time: 83.2 us -> 81.8 us (0.983)
  blocking collectives: 76.7 us -> 75.5 us
    all_to_all x1, blocking collectives: 16 us -> 14.8 us  [shards(): carry = lax.all_to_all(sums, 'seq', 0, 0, axis_index_groups=rows)]
where the time goes in v8:
time: 81.8 us; the launch traced here: 81.5 us
  blocking collectives  75.5 us (92%)
  Pallas kernels  5.3 us (6%)
    all_to_all x1, blocking collectives, shards(): gathered = lax.all_to_all(state, 'seq', 0, 0, axis_index_groups=rows)  25.3 us
    all_to_all x1, blocking collectives, shards(): others = lax.all_to_all(totals, 'seq', 0, 0, axis_index_groups=columns)  20.9 us
    all_to_all x1, blocking collectives, shards(): carry = lax.all_to_all(sums, 'seq', 0, 0, axis_index_groups=rows)  14.8 us
    all_to_all x1, blocking collectives, shards(): parts = lax.all_to_all(send, 'head', 0, 0)  14.5 us
    pallas_call x1, Pallas kernels, shards(): call(functools.partial(grad_out_kernel, full_width), in_specs=[VMEM] * 7,...  2.3 us

profile of v8, /device:TPU:16, one launch (start us, length us, event | category | flops | bytes accessed | tf_op | source)
XLA Modules:
  0.0 81.5 jit_solution(12568601136854364933)
XLA Ops:
  0.6 1.5 %stats.1 = (f32[16,8,128]{2,1,0:T(8,128)S(1)}, bf16[512,384]{1,0:T(8,128)(2,1)S(1)}, bf16[512,384]{1,0:T(8,128)(2,1)S(1)}, f32[384]{0:T(512)S(1)}, bf16[512,384]...) custom-call(bf16[512,384]{1,0:T(8,128)(2,1)} %out_hbm.1, bf16[512,384]{1,0:T(8,128)(2,1)} %grad_hbm.1, ...), custom_call_target="tpu_custom_call" | custom-call | tf_op jit(solution)/shard_map/stats/pallas_call | solution.py:237
  2.2 14.5 %all_to_all.20.parts_ref = f32[16,8,128]{2,1,0:T(8,128)S(1)} all-to-all(f32[16,8,128]{2,1,0:T(8,128)S(1)} %get-tuple-element.15), channel_id=1, replica_groups=mesh['seq'=64,'head'=16] {'head'}, dimensions={0} | all-to-all | bytes 131072 | tf_op jit(solution)/shard_map/all_to_all | solution.py:251
  16.7 2.3 %grad_out.1 = (bf16[512,384]{1,0:T(8,128)(2,1)S(1)}, f32[8,96,128]{2,1,0:T(8,128)S(1)}, f32[384,128]{1,0:T(8,128)S(1)}, f32[384,128]{1,0:T(8,128)S(1)}, f32[3,512,384]{2,1,0:T(8,128)S(1)}) custom-call(f32[16,8,128]{2,1,0:T(8,128)S(1)} %all_to_all.20.parts_ref, bf16[512,384]{1,0:T(8,128)(2,1)S(1)} %get-tuple-element.16.out_ref, ...), custom_call_target="tpu_custom_call" | custom-call | tf_op jit(solution)/shard_map/grad_out/pallas_call | solution.py:252
  19.0 25.3 %all_to_all.21.x_ref = f32[8,96,128]{2,1,0:T(8,128)S(1)} all-to-all(f32[8,96,128]{2,1,0:T(8,128)S(1)} %get-tuple-element.22), channel_id=1, replica_groups={{0,16,32,48,64,80,96,112},{128,144,160,176,192,208,224,240},{256,272,28..., dimensions={0} | all-to-all | bytes 786432 | tf_op jit(solution)/shard_map/all_to_all | solution.py:265
  44.3 20.9 %all_to_all.22.rows_ref = f32[8,48,128]{2,1,0:T(8,128)S(1)} all-to-all(f32[8,48,128]{2,1,0:T(8,128)S(1)} %totals.1), channel_id=1, replica_groups={{0,128,256,384,512,640,768,896},{16,144,272,400,528,656,784,912},{32,16..., dimensions={0} | all-to-all | bytes 393216 | tf_op jit(solution)/shard_map/all_to_all | solution.py:273
  65.2 0.1 sums.1
  65.3 14.8 %all_to_all.23.carry_ref = f32[8,96,128]{2,1,0:T(8,128)S(1)} all-to-all(f32[8,96,128]{2,1,0:T(8,128)S(1)} %sums.1), channel_id=1, replica_groups={{0,16,32,48,64,80,96,112},{128,144,160,176,192,208,224,240},{256,272,28..., dimensions={0} | all-to-all | bytes 786432 | tf_op jit(solution)/shard_map/all_to_all | solution.py:281
  80.1 1.4 %outputs.1 = (bf16[512,384]{1,0:T(8,128)(2,1)}, bf16[512,384]{1,0:T(8,128)(2,1)}, bf16[512,384]{1,0:T(8,128)(2,1)}) custom-call(f32[8,96,128]{2,1,0:T(8,128)S(1)} %all_to_all.23.carry_ref, f32[384,128]{1,0:T(8,128)S(1)} %get-tuple-element.23.kv0_ref, f32[384,128]{1,0:T(8,128)S(1)} %get-tuple-element.24.qg1_ref, ...), custom_call_target="tpu_custom_call" | custom-call | tf_op jit(solution)/shard_map/outputs/pallas_call | solution.py:282
  (1 shorter events, 0.0 us)

commit v9 on v6

--- a/solution.py
+++ b/solution.py
@@ -27,7 +27,7 @@
 
 
 def early():
-    return lax.axis_index("seq") * 8 < lax.axis_size("seq") * 5
+    return lax.rem(lax.axis_index("head"), 2) == 0
 
 
 def within_block(q, k, v, g):

time: 80.8 us -> 80.2 us (level)
    all_to_all x1, blocking collectives: 21.4 us -> 20.5 us  [shards(): carry = lax.all_to_all(scanned.reshape(n_seq, 1, piece), 'seq', 0, 0)]
where the time goes in v9:
time: 80.2 us; the launch traced here: 80 us
  blocking collectives  74.1 us (92%)
  Pallas kernels  5.28 us (7%)
    all_to_all x1, blocking collectives, shards(): gathered = lax.all_to_all(state.reshape(n_seq, 1, piece), 'seq', 0, 0)  39 us
    all_to_all x1, blocking collectives, shards(): carry = lax.all_to_all(scanned.reshape(n_seq, 1, piece), 'seq', 0, 0)  20.5 us
    all_to_all x1, blocking collectives, shards(): parts = lax.all_to_all(send, 'head', 0, 0)  14.5 us
    pallas_call x1, Pallas kernels, shards(): call(functools.partial(grad_out_kernel, full_width), in_specs=[VMEM] * 7,...  2.3 us

profile of v9, /device:TPU:16, one launch (start us, length us, event | category | flops | bytes accessed | tf_op | source)
XLA Modules:
  0.0 80.0 jit_solution(4201456157588570249)
XLA Ops:
  0.6 1.5 %stats.1 = (f32[16,8,128]{2,1,0:T(8,128)S(1)}, bf16[512,384]{1,0:T(8,128)(2,1)S(1)}, bf16[512,384]{1,0:T(8,128)(2,1)S(1)}, f32[384]{0:T(512)S(1)}, bf16[512,384]...) custom-call(bf16[512,384]{1,0:T(8,128)(2,1)} %out_hbm.1, bf16[512,384]{1,0:T(8,128)(2,1)} %grad_hbm.1, ...), custom_call_target="tpu_custom_call" | custom-call | tf_op jit(solution)/shard_map/stats/pallas_call | solution.py:199
  2.2 14.5 %all_to_all.15.parts_ref = f32[16,8,128]{2,1,0:T(8,128)S(1)} all-to-all(f32[16,8,128]{2,1,0:T(8,128)S(1)} %get-tuple-element.15), channel_id=1, replica_groups=mesh['seq'=64,'head'=16] {'head'}, dimensions={0} | all-to-all | bytes 131072 | tf_op jit(solution)/shard_map/all_to_all | solution.py:213
  16.7 2.3 %grad_out.1 = (bf16[512,384]{1,0:T(8,128)(2,1)S(1)}, f32[768,128]{1,0:T(8,128)S(1)}, f32[384,128]{1,0:T(8,128)S(1)}, f32[384,128]{1,0:T(8,128)S(1)}, f32[3,512,384]{2,1,0:T(8,128)S(1)}) custom-call(f32[16,8,128]{2,1,0:T(8,128)S(1)} %all_to_all.15.parts_ref, bf16[512,384]{1,0:T(8,128)(2,1)S(1)} %get-tuple-element.16.out_ref, ...), custom_call_target="tpu_custom_call" | custom-call | tf_op jit(solution)/shard_map/grad_out/pallas_call | solution.py:214
  19.0 39.0 %all_to_all.16 = f32[64,1,1536]{2,1,0:T(1,128)S(1)} all-to-all(f32[64,1,1536]{2,1,0:T(1,128)S(1)} %bitcast.7), channel_id=1, replica_groups=mesh['seq'=64,'head'=16] {'seq'}, dimensions={0} | all-to-all | bytes 786432 | tf_op jit(solution)/shard_map/all_to_all | solution.py:228
  58.0 0.1 scan.1
  58.1 20.5 %all_to_all.17 = f32[64,1,1536]{2,1,0:T(1,128)S(1)} all-to-all(f32[64,1,1536]{2,1,0:T(1,128)S(1)} %bitcast.6), channel_id=1, replica_groups=mesh['seq'=64,'head'=16] {'seq'}, dimensions={0} | all-to-all | bytes 786432 | tf_op jit(solution)/shard_map/all_to_all | solution.py:236
  78.6 1.4 %outputs.1 = (bf16[512,384]{1,0:T(8,128)(2,1)}, bf16[512,384]{1,0:T(8,128)(2,1)}, bf16[512,384]{1,0:T(8,128)(2,1)}) custom-call(f32[768,128]{1,0:T(8,128)S(1)} %bitcast.4, f32[384,128]{1,0:T(8,128)S(1)} %get-tuple-element.23.kv0_ref, f32[384,128]{1,0:T(8,128)S(1)} %get-tuple-element.24.qg1_ref, bf16[512,384]{1,0:T(8,128)(2,1)S(1)} %get-tuple-element.19.q_ref, ...), custom_call_target="tpu_custom_call" | custom-call | tf_op jit(solution)/shard_map/outputs/pallas_call | solution.py:237

commit v10 on v9

--- a/solution.py
+++ b/solution.py
@@ -89,27 +89,31 @@
     coef = total[rows:] * (inv * inv * inv) / full_width
     columns = jnp.concatenate([inv, coef], axis=0).T
     gain = gain_ref[...].reshape(1, width)
-    for r in range(rows):
-        here = pl.ds(r * DH, DH)
-        s = grad_ref[here, :].astype(F32) * gain
-        o = out_ref[here, :].astype(F32)
-        g = s * columns[:, r : r + 1] - o * columns[:, rows + r : rows + r + 1]
-        g_ref[here, :] = g.astype(BF16)
     half = heads * DH
 
-    def terms(a_ref, b_ref, h):
-        cols = pl.ds(h * DH, DH)
-        return [dot(a_ref[pl.ds(b * GROUP, GROUP), cols], b_ref[pl.ds(b * GROUP, GROUP), cols], TN) for b in range(2)]
-
+    def term(a_ref, b_ref, b, h):
+        here, cols = pl.ds(b * GROUP, GROUP), pl.ds(h * DH, DH)
+        return dot(a_ref[here, cols], b_ref[here, cols], TN)
+
+    qg = []
+    for b in range(2):
+        qg.append([])
+        for h in range(heads):
+            cols = pl.ds(h * DH, DH)
+            for r in range(b * rows // 2, (b + 1) * rows // 2):
+                here = pl.ds(r * DH, DH)
+                s = grad_ref[here, cols].astype(F32) * gain[:, h * DH : (h + 1) * DH]
+                o = out_ref[here, cols].astype(F32)
+                g = s * columns[:, r : r + 1] - o * columns[:, rows + r : rows + r + 1]
+                g_ref[here, cols] = g.astype(BF16)
+            qg[b].append(term(q_ref, g_ref, b, h))
     for h in range(heads):
-        qg = terms(q_ref, g_ref, h)
-        qg1_ref[pl.ds(h * DH, DH), :] = qg[1]
-        state_ref[pl.ds(half + h * DH, DH), :] = qg[0] + qg[1]
+        qg1_ref[pl.ds(h * DH, DH), :] = qg[1][h]
+        state_ref[pl.ds(half + h * DH, DH), :] = qg[0][h] + qg[1][h]
     for h in range(heads):
-        kv = terms(k_ref, v_ref, h)
+        kv = [term(k_ref, v_ref, b, h) for b in range(2)]
         kv0_ref[pl.ds(h * DH, DH), :] = kv[0]
         state_ref[pl.ds(h * DH, DH), :] = kv[0] + kv[1]
-
 
     @pl.when(early())
     def _():

time: 80.2 us -> 80.2 us (level)
  no operation moved by 1% of the time
where the time goes in v10:
time: 80.2 us; the launch traced here: 80 us
  blocking collectives  74.1 us (92%)
  Pallas kernels  5.26 us (7%)
    all_to_all x1, blocking collectives, shards(): gathered = lax.all_to_all(state.reshape(n_seq, 1, piece), 'seq', 0, 0)  39 us
    all_to_all x1, blocking collectives, shards(): carry = lax.all_to_all(scanned.reshape(n_seq, 1, piece), 'seq', 0, 0)  20.5 us
    all_to_all x1, blocking collectives, shards(): parts = lax.all_to_all(send, 'head', 0, 0)  14.5 us
    pallas_call x1, Pallas kernels, shards(): call(functools.partial(grad_out_kernel, full_width), in_specs=[VMEM] * 7,...  2.29 us

profile of v10, /device:TPU:16, one launch (start us, length us, event | category | flops | bytes accessed | tf_op | source)
XLA Modules:
  0.0 80.0 jit_solution(10693642103874773024)
XLA Ops:
  0.6 1.5 %stats.1 = (f32[16,8,128]{2,1,0:T(8,128)S(1)}, bf16[512,384]{1,0:T(8,128)(2,1)S(1)}, bf16[512,384]{1,0:T(8,128)(2,1)S(1)}, f32[384]{0:T(512)S(1)}, bf16[512,384]...) custom-call(bf16[512,384]{1,0:T(8,128)(2,1)} %out_hbm.1, bf16[512,384]{1,0:T(8,128)(2,1)} %grad_hbm.1, ...), custom_call_target="tpu_custom_call" | custom-call | tf_op jit(solution)/shard_map/stats/pallas_call | solution.py:203
  2.2 14.5 %all_to_all.15.parts_ref = f32[16,8,128]{2,1,0:T(8,128)S(1)} all-to-all(f32[16,8,128]{2,1,0:T(8,128)S(1)} %get-tuple-element.15), channel_id=1, replica_groups=mesh['seq'=64,'head'=16] {'head'}, dimensions={0} | all-to-all | bytes 131072 | tf_op jit(solution)/shard_map/all_to_all | solution.py:217
  16.7 2.3 %grad_out.1 = (bf16[512,384]{1,0:T(8,128)(2,1)S(1)}, f32[768,128]{1,0:T(8,128)S(1)}, f32[384,128]{1,0:T(8,128)S(1)}, f32[384,128]{1,0:T(8,128)S(1)}, f32[3,512,384]{2,1,0:T(8,128)S(1)}) custom-call(f32[16,8,128]{2,1,0:T(8,128)S(1)} %all_to_all.15.parts_ref, bf16[512,384]{1,0:T(8,128)(2,1)S(1)} %get-tuple-element.16.out_ref, ...), custom_call_target="tpu_custom_call" | custom-call | tf_op jit(solution)/shard_map/grad_out/pallas_call | solution.py:218
  19.0 39.0 %all_to_all.16 = f32[64,1,1536]{2,1,0:T(1,128)S(1)} all-to-all(f32[64,1,1536]{2,1,0:T(1,128)S(1)} %bitcast.7), channel_id=1, replica_groups=mesh['seq'=64,'head'=16] {'seq'}, dimensions={0} | all-to-all | bytes 786432 | tf_op jit(solution)/shard_map/all_to_all | solution.py:232
  58.0 0.1 scan.1
  58.1 20.5 %all_to_all.17 = f32[64,1,1536]{2,1,0:T(1,128)S(1)} all-to-all(f32[64,1,1536]{2,1,0:T(1,128)S(1)} %bitcast.6), channel_id=1, replica_groups=mesh['seq'=64,'head'=16] {'seq'}, dimensions={0} | all-to-all | bytes 786432 | tf_op jit(solution)/shard_map/all_to_all | solution.py:240
  78.6 1.4 %outputs.1 = (bf16[512,384]{1,0:T(8,128)(2,1)}, bf16[512,384]{1,0:T(8,128)(2,1)}, bf16[512,384]{1,0:T(8,128)(2,1)}) custom-call(f32[768,128]{1,0:T(8,128)S(1)} %bitcast.4, f32[384,128]{1,0:T(8,128)S(1)} %get-tuple-element.23.kv0_ref, f32[384,128]{1,0:T(8,128)S(1)} %get-tuple-element.24.qg1_ref, bf16[512,384]{1,0:T(8,128)(2,1)S(1)} %get-tuple-element.19.q_ref, ...), custom_call_target="tpu_custom_call" | custom-call | tf_op jit(solution)/shard_map/outputs/pallas_call | solution.py:241
